TPU v7x, 1024 devices: a whole 8x8x8 slice. The times are simulated.
1024 devices in a mesh: grp: 4 (over y_hi), blk: 32 (over x, y_lo, core), dep: 8 (over z).
Axes of the slice: x: 8, y: 8 (y_hi: 4, y_lo: 2; y = y_hi * 2 + y_lo), z: 8, core: 2. Of those that a mesh axis runs over, the one named last changes fastest.
Arguments:
- velocity: float32 [3, 1024, 64, 128], P(None, 'blk', 'dep', 'grp'), may hold values from -6 to 6
- scalar: float32 [64, 128, 8192], P('dep', 'grp', 'blk'), may hold values from -6 to 6
- spline_base: int32 [8192], P('blk'), may hold values from -1 to 1023, as said below
- spline_frac: float32 [8192], P('blk'), may hold values from 0 to 1
Outputs:
- segment_velocity: float32 [3, 1024, 64, 128], P(None, 'blk', 'dep', 'grp')
- scalar_segment: float32 [64, 128, 8192], P('dep', 'grp', 'blk')
Inputs may be any that keep to these rules, and one draw needn't show every extreme that they name: spline_base[i] is i // 8 or i // 8 - 1; the spline reads velocity cells spline_base[i] - 1 to spline_base[i] + 2 modulo 1024.
All inputs are finite; a program needn't handle non-finite values.
Results may differ from a plain program's by a relative error of at most 0.00007.
Values sent between devices are 32-bit elements; how exact they have to be, the bound alone decides.
A program may use at most 64 MiB of HBM per device.

v0:
```python
import math

import jax
import jax.numpy as jnp
from jax import lax
from jax.sharding import PartitionSpec as P

velocity_step = 0.002
viscosity = 0.00125
advect_rate = 0.2
diffuse_rate = 0.05
first_coeffs = (1.0 / 280.0, -4.0 / 105.0, 0.2, -0.8, 0.0, 0.8, -0.2, 4.0 / 105.0, -1.0 / 280.0)
second_coeffs = (
    -1.0 / 560.0,
    8.0 / 315.0,
    -0.2,
    1.6,
    -205.0 / 72.0,
    1.6,
    -0.2,
    8.0 / 315.0,
    -1.0 / 560.0,
)
highest = lax.Precision.HIGHEST


def padded_2(block, sides, width):
    for axis, dim in sides:
        count = lax.axis_size(axis)
        forward = [(i, i + 1) for i in range(count - 1)]
        forward.append((count - 1, 0))
        backward = [(target, source) for source, target in forward]
        low = lax.ppermute(
            lax.slice_in_dim(block, block.shape[dim] - width, None, axis=dim), axis, forward
        )
        high = lax.ppermute(lax.slice_in_dim(block, 0, width, axis=dim), axis, backward)
        block = jnp.concatenate([low, block, high], axis=dim)
    return block


def derivative_rows(first_row, count, length):
    rows = first_row + lax.iota(jnp.int32, count)
    columns = lax.iota(jnp.int32, length)
    offset = (rows[:, None] - columns[None, :]) % length
    signed = jnp.where(offset > length // 2, offset - length, offset)
    angle = signed.astype(jnp.float32) * (math.pi / length)
    parity = 1.0 - 2.0 * (offset % 2).astype(jnp.float32)
    same = offset == 0
    sine = jnp.where(same, 1.0, jnp.sin(angle))
    first = jnp.where(same, 0.0, 0.5 * parity * jnp.cos(angle) / sine)
    second = jnp.where(same, -(length * length) / 12.0 - 1.0 / 6.0, -0.5 * parity / (sine * sine))
    average = jnp.full((count, length), 1.0 / length, jnp.float32)
    return jnp.concatenate([first, second, average], axis=0)


def catmull_weights(fraction):
    square = fraction * fraction
    cube = square * fraction
    return (
        (-cube + 2.0 * square - fraction) * 0.5,
        (3.0 * cube - 5.0 * square + 2.0) * 0.5,
        (-3.0 * cube + 4.0 * square + fraction) * 0.5,
        (cube - square) * 0.5,
    )


def scalar_update(padded, fine):
    extent = (padded.shape[0] - 8, padded.shape[1] - 8, padded.shape[2] - 8)
    centre = lax.slice(padded, (4, 4, 4), (4 + extent[0], 4 + extent[1], 4 + extent[2]))
    gradients = []
    curvature = jnp.zeros(extent, jnp.float32)
    for axis_index in range(3):
        slope = jnp.zeros(extent, jnp.float32)
        for offset in range(9):
            begin = [4, 4, 4]
            begin[axis_index] = offset
            finish = (begin[0] + extent[0], begin[1] + extent[1], begin[2] + extent[2])
            window = lax.slice(padded, tuple(begin), finish)
            if first_coeffs[offset] != 0.0:
                slope = slope + first_coeffs[offset] * window
            curvature = curvature + second_coeffs[offset] * window
        gradients.append(slope)
    advection = fine[2] * gradients[0] + fine[1] * gradients[1] + fine[0] * gradients[2]
    return centre - advect_rate * advection + diffuse_rate * curvature


def per_device(velocity, scalar, spline_base, spline_frac):
    cells = velocity.shape[1]
    length = cells * lax.axis_size("blk")
    block = lax.axis_index("blk")
    table = derivative_rows(block * cells, cells, length)
    both = jnp.einsum(
        "km,cmzy->ckzy",
        table,
        lax.all_gather(velocity, "blk", axis=1, tiled=True),
        precision=highest,
    )
    segment = (
        velocity
        - both[:, 2 * cells :]
        + velocity_step * (viscosity * both[:, cells : 2 * cells] - velocity[0:1] * both[:, :cells])
    )
    widened = padded_2(segment, (("blk", 1),), 2)
    weights = catmull_weights(spline_frac)
    local_base = spline_base - (block * cells - 2)
    slots = lax.iota(jnp.int32, cells + 4)[:, None]
    matrix = jnp.zeros((cells + 4, spline_base.shape[0]), jnp.float32)
    for tap_index in range(4):
        matrix = matrix + jnp.where(
            slots == (local_base + (tap_index - 1))[None, :], weights[tap_index][None, :], 0.0
        )
    fine = jnp.einsum("cxzy,xi->czyi", widened, matrix, precision=highest)
    padded = padded_2(scalar, (("grp", 1), ("blk", 2), ("dep", 0)), 4)
    return (segment, scalar_update(padded, fine))


def solution(mesh):
    in_specs = (P(None, "blk", "dep", "grp"), P("dep", "grp", "blk"), P("blk"), P("blk"))
    out_specs = (P(None, "blk", "dep", "grp"), P("dep", "grp", "blk"))
    return jax.shard_map(
        per_device, mesh=mesh, in_specs=in_specs, out_specs=out_specs, check_vma=False
    )
```

profile of v0, /device:TPU:1, one launch (start us, length us, event | category | flops | bytes accessed | tf_op | source)
XLA Modules:
  0.0 146.1 jit_solution(4243609040001439258)
XLA Ops:
  7.2 1.8 %copy.10 = f32[3,32,8,32]{3,2,0,1:T(8,128)} copy(f32[3,32,8,32]{3,2,1,0:T(8,128)} %param.4) | data formatting | bytes 196608 | tf_op args[0]
  9.0 0.9 fusion.67
  9.9 7.4 %collective-permute-start.3 = (f32[8,4,256]{2,1,0:T(4,128)S(1)}, f32[8,4,256]{2,1,0:T(4,128)S(1)}, u32[]{:S(2)}, u32[]{:S(2)}) collective-permute-start(f32[8,4,256]{2,1,0:T(4,128)S(1)} %get-tuple-element.19), channel_id=1, source_target_pairs={{256,0},{512,256},{768,512},{0,768},{257,1},{513,257},{769,513},{1... | collective-permute-start | bytes 98312 | tf_op jit(solution)/shard_map/ppermute | solution.py:36
  17.3 1.9 %collective-permute-start.2 = (f32[8,4,256]{2,1,0:T(4,128)S(1)}, f32[8,4,256]{2,1,0:T(4,128)S(1)}, u32[]{:S(2)}, u32[]{:S(2)}) collective-permute-start(f32[8,4,256]{2,1,0:T(4,128)S(1)} %get-tuple-element.18), channel_id=1, source_target_pairs={{0,256},{256,512},{512,768},{768,0},{1,257},{257,513},{513,769},{7... | collective-permute-start | bytes 98312 | tf_op jit(solution)/shard_map/ppermute | solution.py:33
  19.3 0.7 broadcast_add_fusion.2
  20.0 0.7 subtract_multiply_fusion.1
  20.7 0.9 slice_bitcast_fusion.3
  21.6 1.4 divide_select_fusion.1
  23.0 1.0 constant_dynamic-update-slice_fusion.1
  24.0 1.9 %copy.12 = f32[3,32,8,32]{1,3,2,0:T(8,128)} copy(f32[3,32,8,32]{3,2,1,0:T(8,128)} %param.4) | data formatting | bytes 196608 | tf_op args[0]
  25.9 0.8 copy.13
  26.9 3.3 %collective-permute-start.4 = (f32[8,40,4]{2,1,0:T(8,128)S(1)}, f32[8,40,4]{2,1,0:T(8,128)S(1)}, u32[]{:S(2)}, u32[]{:S(2)}) collective-permute-start(f32[8,40,4]{2,1,0:T(8,128)S(1)} %get-tuple-element.16), channel_id=1, source_target_pairs={{0,8},{8,16},{16,24},{24,32},{32,40},{40,48},{48,56},{56,64},{64,7... | collective-permute-start | bytes 15368 | tf_op jit(solution)/shard_map/ppermute | solution.py:33
  30.2 12.1 %collective-permute-start.5 = (f32[8,40,4]{2,1,0:T(8,128)S(1)}, f32[8,40,4]{2,1,0:T(8,128)S(1)}, u32[]{:S(2)}, u32[]{:S(2)}) collective-permute-start(f32[8,40,4]{2,1,0:T(8,128)S(1)} %get-tuple-element.17), channel_id=1, source_target_pairs={{8,0},{16,8},{24,16},{32,24},{40,32},{48,40},{56,48},{64,56},{72,6... | collective-permute-start | bytes 15368 | tf_op jit(solution)/shard_map/ppermute | solution.py:36
  42.4 1.0 collective-permute-done.5
  43.3 0.3 pad_maximum_fusion.1
  43.6 0.8 fusion.64
  44.4 1.9 %collective-permute-start.6 = (f32[4,40,264]{2,1,0:T(8,128)}, f32[4,40,264]{2,1,0:T(8,128)}, u32[]{:S(2)}, u32[]{:S(2)}) collective-permute-start(f32[4,40,264]{2,1,0:T(8,128)} %get-tuple-element.10), channel_id=1, source_target_pairs={{0,1},{1,2},{2,3},{3,4},{4,5},{5,6},{6,7},{7,0},{8,9},{9,10},{10,1... | collective-permute-start | bytes 506888 | tf_op jit(solution)/shard_map/ppermute | solution.py:33
  46.4 15.5 %collective-permute-start.7 = (f32[4,40,264]{2,1,0:T(8,128)}, f32[4,40,264]{2,1,0:T(8,128)}, u32[]{:S(2)}, u32[]{:S(2)}) collective-permute-start(f32[4,40,264]{2,1,0:T(8,128)} %get-tuple-element.11), channel_id=1, source_target_pairs={{1,0},{2,1},{3,2},{4,3},{5,4},{6,5},{7,6},{0,7},{9,8},{10,9},{11,1... | collective-permute-start | bytes 506888 | tf_op jit(solution)/shard_map/ppermute | solution.py:36
  61.9 1.2 maximum_maximum_fusion.1
  63.2 46.4 %all-gather.2.cloned.1.call-done = f32[3,1024,8,32]{3,2,0,1:T(8,128)} async-done(((f32[3,32,8,32]{3,2,0,1:T(8,128)}), f32[3,1024,8,32]{3,2,0,1:T(8,128)}) %all-gather.2.cloned.1.call-update) | async-done | bytes 3145744 | tf_op jit(solution)/shard_map/all_gather | solution.py:95
  109.6 7.5 %copy.11 = f32[3,1024,8,32]{1,3,2,0:T(8,128)S(1)} copy(f32[3,1024,8,32]{3,2,0,1:T(8,128)} %all-gather.2.cloned.1.call-done) | data formatting | bytes 6291456 | tf_op jit(solution)/shard_map/all_gather | solution.py:95
  117.1 3.7 %fusion.3 = f32[96,768]{0,1:S(1)} fusion(f32[1024,768]{0,1:T(8,128)S(1)} %bitcast.40, f32[32,1024]{1,0:T(8,128)} %get-tuple-element.27, f32[32,1024]{1,0:T(8,128)} %get-tuple-element.26, f32[96]{0:T(128)S(1)} %pad.35.clone), kind=kOutput, calls=%fused_computation.14 | convolution fusion | flops 906166272 | bytes 3703168
  120.9 0.3 fusion.2
  121.2 1.0 fusion.65
  122.2 2.2 %collective-permute-start.1 = (f32[3,2,8,32]{1,3,2,0:T(8,128)}, f32[3,2,8,32]{1,3,2,0:T(8,128)}, u32[]{:S(2)}, u32[]{:S(2)}) collective-permute-start(f32[3,2,8,32]{1,3,2,0:T(8,128)} %get-tuple-element.13), channel_id=1, source_target_pairs={{8,0},{16,8},{24,16},{32,24},{40,32},{48,40},{56,48},{64,56},{72,6... | collective-permute-start | bytes 18440 | tf_op jit(solution)/shard_map/ppermute | solution.py:36
  124.4 3.4 %collective-permute-start = (f32[3,2,8,32]{1,3,2,0:T(8,128)}, f32[3,2,8,32]{1,3,2,0:T(8,128)}, u32[]{:S(2)}, u32[]{:S(2)}) collective-permute-start(f32[3,2,8,32]{1,3,2,0:T(8,128)} %get-tuple-element.12), channel_id=1, source_target_pairs={{0,8},{8,16},{16,24},{24,32},{32,40},{40,48},{48,56},{56,64},{64,7... | collective-permute-start | bytes 18440 | tf_op jit(solution)/shard_map/ppermute | solution.py:33
  127.8 1.6 %maximum_maximum_fusion = (f32[12,40,264]{2,1,0:T(8,128)S(1)}, f32[12,40,264]{2,1,0:T(8,128)S(1)}) fusion(f32[8,40,4]{2,1,0:T(8,128)S(1)} %copy-done.9, f32[8,4,256]{2,1,0:T(4,128)S(1)} %collective-permute-done.3, f32[8,32,256]{2,1,0:T(8,128)S(1)} %copy-done, f32[8,4,256]{2,1,0:T(4,128)S(1)} %collective-permute-done.2, f32[8,40,4]{2,1,0:T(8,128)S(1)} %copy-done.7, ...), kind=kLoop, calls=%fused_computation | loop fusion | flops 1267200 | bytes 1689600 | tf_op jit(solution)/shard_map/concatenate | solution.py:37
  129.4 0.9 copy.14
  130.3 1.3 collective-permute-done.1
  131.6 3.6 %collective-permute-done = f32[3,2,8,32]{1,3,2,0:T(8,128)} collective-permute-done((f32[3,2,8,32]{1,3,2,0:T(8,128)}, f32[3,2,8,32]{1,3,2,0:T(8,128)}, u32[]{:S(2)}, u32[]{:S(2)}) %collective-permute-start) | collective-permute-done | bytes 6176 | tf_op jit(solution)/shard_map/ppermute | solution.py:33
  135.2 1.9 %fusion.8 = f32[3,8,32,256]{3,2,1,0:T(8,128)S(1)} fusion(f32[3,2,8,32]{1,3,2,0:T(8,128)} %collective-permute-done.1, f32[3,32,8,32]{1,3,2,0:T(8,128)S(1)} %fusion.2, f32[3,2,8,32]{1,3,2,0:T(8,128)} %collective-permute-done, f32[256]{0:T(256)S(1)} %get-tuple-element.21, s32[256]{0:T(256)S(1)} %get-tuple-element.25, f32[256]{0:T(256)S(1)} %get-tuple-element.23, ...), kind=kOutput, calls=%fused_computation.19 | convolution fusion | flops 85091328 | bytes 905216 | tf_op jit(solution)/shard_map/cxzy,xi->czyi/dot_general | solution.py:112
  137.2 2.1 %fusion.21 = f32[8,32,256]{2,1,0:T(8,128)} fusion(f32[8,32,256]{2,1,0:T(8,128)S(1)} %copy-done, f32[3,8,32,256]{3,2,1,0:T(8,128)S(1)} %fusion.8, f32[8,40,260]{2,1,0:T(8,128)S(1)} %copy-done.4, f32[8,40,260]{2,1,0:T(8,128)S(1)} %copy-done.3, f32[8,36,256]{2,1,0:T(8,128)S(1)} %copy-done.2, f32[8,4,256]{2,1,0:T(4,128)S(1)} %collective-permute-done.2, ...), kind=kLoop, calls=%fused_computation.39 | loop fusion | flops 6946816 | bytes 6586368 | tf_op jit(solution)/shard_map/add | solution.py:84
  (36 shorter events, 0.4 us)
Async XLA Ops:
  7.2 19.6 %copy-start = (f32[8,32,256]{2,1,0:T(8,128)S(1)}, f32[8,32,256]{2,1,0:T(8,128)}, u32[]{:S(2)}) copy-start(f32[8,32,256]{2,1,0:T(8,128)} %param.5) | copy-start | bytes 786436
  7.2 102.4 %all-gather.2.cloned.1.call-start = ((), (), s32[]{:S(2)}) async-start(), calls=%async_computation | async-start | bytes 12976128 | tf_op jit(solution)/shard_map/all_gather | solution.py:95
  9.9 16.8 %collective-permute-start.3 = (f32[8,4,256]{2,1,0:T(4,128)S(1)}, f32[8,4,256]{2,1,0:T(4,128)S(1)}, u32[]{:S(2)}, u32[]{:S(2)}) collective-permute-start(f32[8,4,256]{2,1,0:T(4,128)S(1)} %get-tuple-element.19), channel_id=1, source_target_pairs={{256,0},{512,256},{768,512},{0,768},{257,1},{513,257},{769,513},{1... | collective-permute-start | bytes 98312 | tf_op jit(solution)/shard_map/ppermute | solution.py:36
  17.3 9.4 %collective-permute-start.2 = (f32[8,4,256]{2,1,0:T(4,128)S(1)}, f32[8,4,256]{2,1,0:T(4,128)S(1)}, u32[]{:S(2)}, u32[]{:S(2)}) collective-permute-start(f32[8,4,256]{2,1,0:T(4,128)S(1)} %get-tuple-element.18), channel_id=1, source_target_pairs={{0,256},{256,512},{512,768},{768,0},{1,257},{257,513},{513,769},{7... | collective-permute-start | bytes 98312 | tf_op jit(solution)/shard_map/ppermute | solution.py:33
  26.9 15.4 %collective-permute-start.4 = (f32[8,40,4]{2,1,0:T(8,128)S(1)}, f32[8,40,4]{2,1,0:T(8,128)S(1)}, u32[]{:S(2)}, u32[]{:S(2)}) collective-permute-start(f32[8,40,4]{2,1,0:T(8,128)S(1)} %get-tuple-element.16), channel_id=1, source_target_pairs={{0,8},{8,16},{16,24},{24,32},{32,40},{40,48},{48,56},{56,64},{64,7... | collective-permute-start | bytes 15368 | tf_op jit(solution)/shard_map/ppermute | solution.py:33
  30.2 13.1 %collective-permute-start.5 = (f32[8,40,4]{2,1,0:T(8,128)S(1)}, f32[8,40,4]{2,1,0:T(8,128)S(1)}, u32[]{:S(2)}, u32[]{:S(2)}) collective-permute-start(f32[8,40,4]{2,1,0:T(8,128)S(1)} %get-tuple-element.17), channel_id=1, source_target_pairs={{8,0},{16,8},{24,16},{32,24},{40,32},{48,40},{56,48},{64,56},{72,6... | collective-permute-start | bytes 15368 | tf_op jit(solution)/shard_map/ppermute | solution.py:36
  42.3 20.8 %copy-start.1 = (f32[8,36,256]{2,1,0:T(8,128)}, f32[8,36,256]{2,1,0:T(8,128)S(1)}, u32[]{:S(2)}) copy-start(f32[8,36,256]{2,1,0:T(8,128)S(1)} %constant_dynamic-update-slice_fusion) | copy-start | bytes 884740
  42.3 19.6 %copy-start.6 = (f32[8,40,4]{2,1,0:T(8,128)}, f32[8,40,4]{2,1,0:T(8,128)S(1)}, u32[]{:S(2)}) copy-start(f32[8,40,4]{2,1,0:T(8,128)S(1)} %collective-permute-done.4) | copy-start | bytes 15364
  43.3 18.6 %copy-start.8 = (f32[8,40,4]{2,1,0:T(8,128)}, f32[8,40,4]{2,1,0:T(8,128)S(1)}, u32[]{:S(2)}) copy-start(f32[8,40,4]{2,1,0:T(8,128)S(1)} %collective-permute-done.5) | copy-start | bytes 15364
  44.4 83.3 %collective-permute-start.6 = (f32[4,40,264]{2,1,0:T(8,128)}, f32[4,40,264]{2,1,0:T(8,128)}, u32[]{:S(2)}, u32[]{:S(2)}) collective-permute-start(f32[4,40,264]{2,1,0:T(8,128)} %get-tuple-element.10), channel_id=1, source_target_pairs={{0,1},{1,2},{2,3},{3,4},{4,5},{5,6},{6,7},{7,0},{8,9},{9,10},{10,1... | collective-permute-start | bytes 506888 | tf_op jit(solution)/shard_map/ppermute | solution.py:33
  46.4 81.4 %collective-permute-start.7 = (f32[4,40,264]{2,1,0:T(8,128)}, f32[4,40,264]{2,1,0:T(8,128)}, u32[]{:S(2)}, u32[]{:S(2)}) collective-permute-start(f32[4,40,264]{2,1,0:T(8,128)} %get-tuple-element.11), channel_id=1, source_target_pairs={{1,0},{2,1},{3,2},{4,3},{5,4},{6,5},{7,6},{0,7},{9,8},{10,9},{11,1... | collective-permute-start | bytes 506888 | tf_op jit(solution)/shard_map/ppermute | solution.py:36
  117.1 3.8 %copy-start.5 = (f32[3,32,8,32]{1,3,2,0:T(8,128)S(1)}, f32[3,32,8,32]{1,3,2,0:T(8,128)}, u32[]{:S(2)}) copy-start(f32[3,32,8,32]{1,3,2,0:T(8,128)} %copy.12) | copy-start | bytes 294916
  117.1 3.8 %copy-start.10 = (f32[32,8,32]{0,2,1:T(8,128)S(1)}, f32[32,8,32]{0,2,1:T(8,128)}, u32[]{:S(2)}) copy-start(f32[32,8,32]{0,2,1:T(8,128)} %copy.13) | copy-start | bytes 98308
  117.1 10.7 %copy-start.7 = (f32[8,40,4]{2,1,0:T(8,128)S(1)}, f32[8,40,4]{2,1,0:T(8,128)}, u32[]{:S(2)}) copy-start(f32[8,40,4]{2,1,0:T(8,128)} %copy-done.6) | copy-start | bytes 15364
  117.1 10.7 %copy-start.9 = (f32[8,40,4]{2,1,0:T(8,128)S(1)}, f32[8,40,4]{2,1,0:T(8,128)}, u32[]{:S(2)}) copy-start(f32[8,40,4]{2,1,0:T(8,128)} %copy-done.8) | copy-start | bytes 15364
  121.1 16.0 %copy-start.2 = (f32[8,36,256]{2,1,0:T(8,128)S(1)}, f32[8,36,256]{2,1,0:T(8,128)}, u32[]{:S(2)}) copy-start(f32[8,36,256]{2,1,0:T(8,128)} %copy-done.1) | copy-start | bytes 884740
  121.1 16.0 %copy-start.3 = (f32[8,40,260]{2,1,0:T(8,128)S(1)}, f32[8,40,260]{2,1,0:T(8,128)}, u32[]{:S(2)}) copy-start(f32[8,40,260]{2,1,0:T(8,128)} %get-tuple-element.14) | copy-start | bytes 998404
  121.1 16.0 %copy-start.4 = (f32[8,40,260]{2,1,0:T(8,128)S(1)}, f32[8,40,260]{2,1,0:T(8,128)}, u32[]{:S(2)}) copy-start(f32[8,40,260]{2,1,0:T(8,128)} %get-tuple-element.15) | copy-start | bytes 998404
  122.2 9.4 %collective-permute-start.1 = (f32[3,2,8,32]{1,3,2,0:T(8,128)}, f32[3,2,8,32]{1,3,2,0:T(8,128)}, u32[]{:S(2)}, u32[]{:S(2)}) collective-permute-start(f32[3,2,8,32]{1,3,2,0:T(8,128)} %get-tuple-element.13), channel_id=1, source_target_pairs={{8,0},{16,8},{24,16},{32,24},{40,32},{48,40},{56,48},{64,56},{72,6... | collective-permute-start | bytes 18440 | tf_op jit(solution)/shard_map/ppermute | solution.py:36
  124.4 10.8 %collective-permute-start = (f32[3,2,8,32]{1,3,2,0:T(8,128)}, f32[3,2,8,32]{1,3,2,0:T(8,128)}, u32[]{:S(2)}, u32[]{:S(2)}) collective-permute-start(f32[3,2,8,32]{1,3,2,0:T(8,128)} %get-tuple-element.12), channel_id=1, source_target_pairs={{0,8},{8,16},{16,24},{24,32},{32,40},{40,48},{48,56},{56,64},{64,7... | collective-permute-start | bytes 18440 | tf_op jit(solution)/shard_map/ppermute | solution.py:33
Sparse Core Ops, SparseCore 0:
  11.3 98.2 all-gather.1
where the time goes:
time: 148 us; the launch traced here: 146 us
  waiting for transfers between devices  52.3 us (35%)
  starting transfers between devices  47.7 us (32%)
  local copies, waits for them, and re-layouts  17.8 us (12%)
  between operations  14.4 us (10%)
  other arithmetic  8.33 us (6%)
  matrix products  5.64 us (4%)
    all_gather x1, waiting for transfers between devices, per_device(): lax.all_gather(velocity, 'blk', axis=1, tiled=True)  46.4 us
    ppermute x4, starting transfers between devices, padded_2(): lax.ppermute(lax.slice_in_dim(block, 0, width, axis=dim), axis, backward)  37.2 us
    ppermute x4, starting transfers between devices, padded_2(): lax.ppermute(lax.slice_in_dim(block, block.shape[dim] - width, None, axis...  10.5 us
    all_gather x1, local copies, waits for them, and re-layouts, per_device(): lax.all_gather(velocity, 'blk', axis=1, tiled=True)  7.51 us
    unnamed x26, local copies, waits for them, and re-layouts  5.66 us
    unnamed x1, matrix products  3.71 us
    ppermute x4, waiting for transfers between devices, padded_2(): lax.ppermute(lax.slice_in_dim(block, block.shape[dim] - width, None, axis...  3.6 us
    concatenate x4, other arithmetic, padded_2(): block = jnp.concatenate([low, block, high], axis=dim)  3.13 us
  transfers between devices with their start and end apart: 9, of which 4 were waited for; matrix products, arithmetic and copies ran while one was open for 18% of the time, Pallas kernels for 0%

commit v1 on v0

v1 whole, which is shorter than its diff:
```python
import math

import jax
import jax.numpy as jnp
import numpy as np
from jax import lax
from jax.experimental import pallas as pl
from jax.experimental.pallas import tpu as pltpu
from jax.sharding import PartitionSpec as P

velocity_step = 0.002
viscosity = 0.00125
advect_rate = 0.2
diffuse_rate = 0.05
first_coeffs = (0.8, -0.2, 4.0 / 105.0, -1.0 / 280.0)
second_coeffs = (1.6, -0.2, 8.0 / 315.0, -1.0 / 560.0)
second_centre = -205.0 / 72.0

LENGTH = 1024
GROUP = 32
TILE = 256
f32, bf16 = jnp.float32, jnp.bfloat16


def spectral_tables():
    offset = (np.arange(LENGTH)[None, :] - np.arange(TILE)[:, None]) % LENGTH
    angle = np.pi * offset / LENGTH
    parity = 1.0 - 2.0 * (offset % 2)
    same = offset == 0
    sine = np.where(same, 1.0, np.sin(angle))
    first = np.where(same, 0.0, 0.5 * parity * np.cos(angle) / sine)
    second = np.where(same, -(LENGTH**2) / 12.0 - 1.0 / 6.0, -0.5 * parity / sine**2)
    table = np.concatenate([velocity_step * first, velocity_step * viscosity * second], axis=1)
    high = table.astype(np.float32).astype(jnp.bfloat16)
    low = (table - high.astype(np.float64)).astype(np.float32).astype(jnp.bfloat16)
    return np.concatenate([high, low], axis=1)


def split(value):
    high = value.astype(bf16)
    return high, (value - high.astype(f32)).astype(bf16)


def swap_groups(tiles, lane):
    out = []
    for r in range(4):
        value = tiles[r]
        for c in range(4):
            if c == r:
                continue
            moved = pltpu.roll(tiles[c], (32 * (c - r)) % 128, axis=1)
            value = jnp.where(lane // 32 == c, moved, value)
        out.append(value)
    return out


def shift_lanes(tiles, amount):
    lane = lax.broadcasted_iota(jnp.int32, (8, 128), 1)
    count = len(tiles)
    rolled = [pltpu.roll(tile, amount % 128, axis=1) for tile in tiles]
    if amount > 0:
        return [jnp.where(lane < amount, rolled[i - 1], rolled[i]) for i in range(count)]
    edge = 128 + amount
    return [jnp.where(lane < edge, rolled[i], rolled[(i + 1) % count]) for i in range(count)]


def pack_velocity(vel, send):
    for z in range(8):
        part = vel[pl.ds(z, 96, stride=8), :]
        part = jnp.concatenate([part, jnp.zeros((32, 32), f32)], axis=0)
        send[pl.ds(z, 32, stride=8), :] = part.T


def spectral_segment(recv, table, rows, raw, prod, send):
    lane = lax.broadcasted_iota(jnp.int32, (8, 128), 1)
    totals = [None] * 3
    for x in range(8):
        tiles = [recv[(4 * x + r) * 8 : (4 * x + r) * 8 + 8, :] for r in range(4)]
        got = swap_groups(tiles, lane)
        for c in range(3):
            raw[c, :, 128 * x : 128 * x + 128] = got[c]
            totals[c] = got[c] if x == 0 else totals[c] + got[c]
    for c in range(3):
        mean = jnp.sum(totals[c], axis=1, keepdims=True) * (1.0 / LENGTH)
        for j in range(4):
            rows[j * 24 + c * 8 : j * 24 + c * 8 + 8, :] = (
                raw[c, :, TILE * j : TILE * j + TILE] - mean
            )
    high, low = split(rows[...])
    both = jnp.concatenate([high, low], axis=0)
    for m in range(8):
        cols = slice(TILE * m, TILE * m + TILE)
        lows = slice(2 * LENGTH + TILE * m, 2 * LENGTH + TILE * m + TILE)
        main = jnp.dot(both, table[:, cols], preferred_element_type=f32)
        rest = jnp.dot(high, table[:, lows], preferred_element_type=f32)
        prod[:, cols] = main[:96] + main[96:] + rest
    segment = [[], [], []]
    for k in range(4):
        speed = raw[0, :, TILE * k : TILE * k + TILE]
        for c in range(3):
            first = second = None
            for j in range(4):
                m = (k - j) % 4
                at = slice(j * 24 + c * 8, j * 24 + c * 8 + 8)
                a = prod[at, TILE * m : TILE * m + TILE]
                b = prod[at, LENGTH + TILE * m : LENGTH + TILE * m + TILE]
                first = a if j == 0 else first + a
                second = b if j == 0 else second + b
            own = rows[k * 24 + c * 8 : k * 24 + c * 8 + 8, :]
            value = own + (second - speed * first)
            segment[c] += [value[:, :128], value[:, 128:]]
    within = lane % 32
    halo = [jnp.zeros((8, 128), f32)] * 8
    for c in range(3):
        low_side = shift_lanes(segment[c], 2 + 4 * c)
        high_side = shift_lanes(segment[c], -30 + 4 * c)
        for x in range(8):
            halo[x] = jnp.where(within // 2 == 2 * c, low_side[x], halo[x])
            halo[x] = jnp.where(within // 2 == 2 * c + 1, high_side[x], halo[x])
    for x in range(8):
        tiles = swap_groups([segment[0][x], segment[1][x], segment[2][x], halo[x]], lane)
        for r in range(4):
            send[(4 * x + r) * 8 : (4 * x + r) * 8 + 8, :] = tiles[r]


def spline_matrix(base, frac, first_cell):
    row = lax.broadcasted_iota(jnp.int32, (128, TILE), 0)
    side = row - 96
    halo = side % 4
    slot = jnp.where(row < 96, row % 32 + 2, jnp.where(halo < 2, halo, halo + 32))
    owner = jnp.where(row < 96, row // 32, side // 4)
    local = base - (first_cell - 2)
    square = frac * frac
    cube = square * frac
    weights = (
        (-cube + 2.0 * square - frac) * 0.5,
        (3.0 * cube - 5.0 * square + 2.0) * 0.5,
        (-3.0 * cube + 4.0 * square + frac) * 0.5,
        (cube - square) * 0.5,
    )
    matrix = jnp.zeros((128, TILE), f32)
    for tap in range(4):
        matrix = matrix + jnp.where(slot == local + (tap - 1), weights[tap], 0.0)
    return [jnp.where(owner == c, matrix, 0.0) for c in range(3)]


def pair_sums(window):
    slope = curve = None
    for m in range(1, 5):
        ahead, behind = window(m), window(-m)
        a = first_coeffs[m - 1] * (ahead - behind)
        b = second_coeffs[m - 1] * (ahead + behind)
        slope = a if m == 1 else slope + a
        curve = b if m == 1 else curve + b
    return slope, curve


def stencils(sc, zhalo, ypad, xhalo, slopes, still):
    pad = jnp.zeros((120, TILE), f32)
    left = jnp.concatenate([pad, xhalo[0]], axis=0).T
    right = jnp.concatenate([xhalo[1], pad], axis=0).T
    for z in range(8):
        own = sc[z]

        def along_z(m):
            at = z + m
            if at < 0:
                return zhalo[0, 4 + at]
            return zhalo[1, at - 8] if at >= 8 else sc[at]

        def along_y(m):
            return ypad[z, 8 + m : 40 + m, :]

        wide = jnp.concatenate([left[32 * z : 32 * z + 32], own, right[32 * z : 32 * z + 32]], axis=1)

        def along_x(m):
            return pltpu.roll(wide, (-m) % 512, axis=1)[:, 128:384]

        slope_z, curve_z = pair_sums(along_z)
        slope_y, curve_y = pair_sums(along_y)
        slope_x, curve_x = pair_sums(along_x)
        curve = curve_z + curve_y + curve_x + (3.0 * second_centre) * own
        still[z] = own + diffuse_rate * curve
        slopes[0, z] = advect_rate * slope_x
        slopes[1, z] = advect_rate * slope_y
        slopes[2, z] = advect_rate * slope_z


def finish(recv, weights, slopes, still, lhs, seg_out, sc_out):
    for z in range(8):
        tile = recv[pl.ds(z, 32, stride=8), :]
        lhs[32 * z : 32 * z + 32, :] = tile
        seg_out[pl.ds(z, 96, stride=8), :] = tile.T[:96]
    high, low = split(lhs[...])
    both = jnp.concatenate([high, low], axis=1)
    fine = []
    for c in range(3):
        w_high, w_low = split(weights[c])
        fine.append(
            jnp.dot(both, jnp.concatenate([w_high, w_high], axis=0), preferred_element_type=f32)
            + jnp.dot(high, w_low, preferred_element_type=f32)
        )
    for z in range(8):
        at = slice(32 * z, 32 * z + 32)
        moved = fine[0][at] * slopes[0, z] + fine[1][at] * slopes[1, z] + fine[2][at] * slopes[2, z]
        sc_out[z] = still[z] - moved


def kernel(
    vel_in, sc_in, base_in, frac_in, tab_in, seg_out, sc_out,
    vel, sc, tab, send1, recv1, send2, recv2, rows, raw, prod, lhs,
    zhalo, ysend, yhalo, ypad, xsend, xhalo, slopes, still,
    load_sem, a_send, a_recv, b_send, b_recv, h_send, h_recv,
):
    me = lax.axis_index("blk")
    grp, dep = lax.axis_index("grp"), lax.axis_index("dep")
    n_grp, n_dep = lax.axis_size("grp"), lax.axis_size("dep")

    loads = [
        pltpu.make_async_copy(src, dst, load_sem.at[i])
        for i, (src, dst) in enumerate(((vel_in, vel), (sc_in, sc), (tab_in, tab)))
    ]
    for load in loads:
        load.start()

    barrier = pltpu.get_barrier_semaphore()
    near = (
        {"dep": lax.rem(dep + 1, n_dep)},
        {"dep": lax.rem(dep + n_dep - 1, n_dep)},
        {"grp": lax.rem(grp + 1, n_grp)},
        {"grp": lax.rem(grp + n_grp - 1, n_grp)},
        {"blk": lax.rem(me + 1, GROUP)},
        {"blk": lax.rem(me + GROUP - 1, GROUP)},
    )

    def far_first(j):
        half = (j + 1) // 2
        offset = 16 + half * (2 * lax.rem(j, 2) - 1)
        return lax.rem(me + offset, GROUP)

    def greet(j, carry):
        pl.semaphore_signal(barrier, inc=1, device_id={"blk": far_first(j)}, device_id_type=pl.DeviceIdType.MESH)
        return carry

    lax.fori_loop(0, GROUP - 1, greet, 0)
    for peer in near[:4]:
        pl.semaphore_signal(barrier, inc=1, device_id=peer, device_id_type=pl.DeviceIdType.MESH)

    loads[0].wait()
    pack_velocity(vel, send1)
    loads[1].wait()
    for h in range(2):
        ysend[0, :, 4 * h : 4 * h + 4, :] = sc[4 * h : 4 * h + 4, 28:32, :]
        ysend[1, :, 4 * h : 4 * h + 4, :] = sc[4 * h : 4 * h + 4, 0:4, :]
    flat = sc[...].reshape(TILE, TILE)
    xsend[0] = flat[:, 128:].T[120:]
    xsend[1] = flat[:, :128].T[:8]
    pl.semaphore_wait(barrier, GROUP - 1 + 4)

    def exchange(src, dst, send_sem, recv_sem):
        def step(j, carry):
            peer = far_first(j)
            pltpu.make_async_remote_copy(
                src_ref=src.at[pl.ds(pl.multiple_of(peer * 8, 8), 8)],
                dst_ref=dst.at[pl.ds(pl.multiple_of(me * 8, 8), 8)],
                send_sem=send_sem,
                recv_sem=recv_sem,
                device_id={"blk": peer},
                device_id_type=pl.DeviceIdType.MESH,
            ).start()
            return carry

        lax.fori_loop(0, GROUP - 1, step, 0)
        at = pl.ds(pl.multiple_of(me * 8, 8), 8)
        dst[at, :] = src[at, :]

    def settle(buffer, sem):
        part = buffer.at[pl.ds(0, (GROUP - 1) * 8)]
        pltpu.make_async_copy(part, part, sem).wait()

    exchange(send1, recv1, a_send, a_recv)
    halos = []
    pieces = (
        (sc.at[pl.ds(4, 4)], zhalo.at[0]),
        (sc.at[pl.ds(0, 4)], zhalo.at[1]),
        (ysend.at[0], yhalo.at[0]),
        (ysend.at[1], yhalo.at[1]),
        (xsend.at[0], xhalo.at[0]),
        (xsend.at[1], xhalo.at[1]),
    )
    for i, (src, dst) in enumerate(pieces):
        copy = pltpu.make_async_remote_copy(
            src_ref=src, dst_ref=dst, send_sem=h_send.at[i], recv_sem=h_recv.at[i],
            device_id=near[i], device_id_type=pl.DeviceIdType.MESH,
        )
        copy.start()
        halos.append(copy)
    loads[2].wait()
    settle(recv1, a_recv)
    spectral_segment(recv1, tab, rows, raw, prod, send2)
    exchange(send2, recv2, b_send, b_recv)

    weights = spline_matrix(base_in[...], frac_in[...], me * GROUP)
    for copy in halos:
        copy.wait()
    ypad[:, 8:40, :] = sc[...]
    for h in range(2):
        at = slice(4 * h, 4 * h + 4)
        ypad[at, 4:8, :] = yhalo[0, :, at, :]
        ypad[at, 40:44, :] = yhalo[1, :, at, :]
    stencils(sc, zhalo, ypad, xhalo, slopes, still)
    settle(recv2, b_recv)
    finish(recv2, weights, slopes, still, lhs, seg_out, sc_out)
    settle(send1, a_send)
    settle(send2, b_send)


def per_device(velocity, scalar, spline_base, spline_frac):
    vmem = pl.BlockSpec(memory_space=pltpu.VMEM)
    anywhere = pl.BlockSpec(memory_space=pl.ANY)
    tables = jnp.asarray(spectral_tables())
    segment, out = pl.pallas_call(
        kernel,
        out_shape=(
            jax.ShapeDtypeStruct((768, 32), f32),
            jax.ShapeDtypeStruct((8, 32, TILE), f32),
        ),
        in_specs=[anywhere, anywhere, vmem, vmem, anywhere],
        out_specs=(vmem, vmem),
        scratch_shapes=[
            pltpu.VMEM((768, 32), f32),
            pltpu.VMEM((8, 32, TILE), f32),
            pltpu.VMEM((TILE, 4 * LENGTH), bf16),
            pltpu.VMEM((TILE, 128), f32),
            pltpu.VMEM((TILE, 128), f32),
            pltpu.VMEM((TILE, 128), f32),
            pltpu.VMEM((TILE, 128), f32),
            pltpu.VMEM((96, TILE), f32),
            pltpu.VMEM((3, 8, LENGTH), f32),
            pltpu.VMEM((96, 2 * LENGTH), f32),
            pltpu.VMEM((TILE, 128), f32),
            pltpu.VMEM((2, 4, 32, TILE), f32),
            pltpu.VMEM((2, 4, 8, TILE), f32),
            pltpu.VMEM((2, 4, 8, TILE), f32),
            pltpu.VMEM((8, 48, TILE), f32),
            pltpu.VMEM((2, 8, TILE), f32),
            pltpu.VMEM((2, 8, TILE), f32),
            pltpu.VMEM((3, 8, 32, TILE), f32),
            pltpu.VMEM((8, 32, TILE), f32),
            pltpu.SemaphoreType.DMA((3,)),
            pltpu.SemaphoreType.DMA,
            pltpu.SemaphoreType.DMA,
            pltpu.SemaphoreType.DMA,
            pltpu.SemaphoreType.DMA,
            pltpu.SemaphoreType.DMA((6,)),
            pltpu.SemaphoreType.DMA((6,)),
        ],
        compiler_params=pltpu.CompilerParams(collective_id=0, has_side_effects=True),
        name="segment",
    )(
        velocity.reshape(768, 32),
        scalar,
        spline_base.reshape(1, TILE),
        spline_frac.reshape(1, TILE),
        tables,
    )
    return segment.reshape(velocity.shape), out


def solution(mesh):
    in_specs = (P(None, "blk", "dep", "grp"), P("dep", "grp", "blk"), P("blk"), P("blk"))
    out_specs = (P(None, "blk", "dep", "grp"), P("dep", "grp", "blk"))
    return jax.shard_map(
        per_device, mesh=mesh, in_specs=in_specs, out_specs=out_specs, check_vma=False
    )
```

time: 148 us -> 38.6 us (0.26); the launches traced: 146 us -> 38.3 us
  waiting for transfers between devices: 52.3 us -> 0 us
  starting transfers between devices: 47.7 us -> 0 us
  Pallas kernels: 0 us -> 34.2 us
  local copies, waits for them, and re-layouts: 17.8 us -> 3.44 us
  between operations: 14.4 us -> 0.64 us
  other arithmetic: 8.33 us -> 0 us
  matrix products: 5.64 us -> 0 us
    ppermute x8 -> x0, starting transfers between devices: 47.7 us -> none  [the longest x4 37.2 us: padded_2(): lax.ppermute(lax.slice_in_dim(block, 0, width, axis=dim), axis, backward)]
    all_gather x1 -> x0, waiting for transfers between devices: 46.4 us -> none  [per_device(): lax.all_gather(velocity, 'blk', axis=1, tiled=True)]
    pallas_call x0 -> x1, Pallas kernels: none -> 34.2 us  [per_device(): pl.pallas_call(kernel, out_shape=(jax.ShapeDtypeStruct((768, 32), f32), j...]
    all_gather x1 -> x0, local copies, waits for them, and re-layouts: 7.51 us -> none  [per_device(): lax.all_gather(velocity, 'blk', axis=1, tiled=True)]
    ppermute x8 -> x0, waiting for transfers between devices: 5.86 us -> none  [the longest x4 3.6 us: padded_2(): lax.ppermute(lax.slice_in_dim(block, block.shape[dim] - width, None, axis...]
    unnamed x1 -> x0, matrix products: 3.71 us -> none
    concatenate x4 -> x0, other arithmetic: 3.13 us -> none  [padded_2(): block = jnp.concatenate([low, block, high], axis=dim)]
    add x5 -> x0, other arithmetic: 3.08 us -> none  [the longest x1 2.11 us: scalar_update(): return centre - advect_rate * advection + diffuse_rate * curvature]
  transfers between devices with their start and end apart: 9 -> 0, of which waited for: 4 -> 0; matrix products, arithmetic and copies ran while one was open for 18% -> 0% of each run, Pallas kernels for 0% -> 0%
where the time goes in v1:
time: 38.6 us; the launch traced here: 38.3 us
  Pallas kernels  34.2 us (89%)
  local copies, waits for them, and re-layouts  3.44 us (9%)
  between operations  0.64 us (2%)
    pallas_call x1, Pallas kernels, per_device(): pl.pallas_call(kernel, out_shape=(jax.ShapeDtypeStruct((768, 32), f32), j...  34.2 us
    unnamed x2, local copies, waits for them, and re-layouts  3.44 us

profile of v1, /device:TPU:1, one launch (start us, length us, event | category | flops | bytes accessed | tf_op | source)
XLA Modules:
  0.0 38.3 jit_solution(2488828380550734162)
XLA Ops:
  0.6 34.2 %segment.1 = (f32[768,32]{1,0:T(8,128)}, f32[8,32,256]{2,1,0:T(8,128)}) custom-call(f32[768,32]{1,0:T(8,128)} %bitcast.4, f32[8,32,256]{2,1,0:T(8,128)} %sc_in.1, s32[1,256]{1,0:T(1,128)} %bitcast.6, f32[1,256]{1,0:T(1,128)} %bitcast.7, bf16[256,4096]{1,0:T(8,128)(2,1)} %constant.2.clone.tab_in), custom_call_target="tpu_custom_call" | custom-call | tf_op jit(solution)/shard_map/segment/pallas_call | solution.py:322
  34.9 1.8 %copy.9 = f32[3,32,8,32]{3,2,1,0:T(8,128)} copy(f32[3,32,8,32]{3,2,1,0:T(8,128)} %bitcast.5) | data formatting | bytes 196608
  36.7 1.7 %copy.10 = f32[8,32,256]{2,1,0:T(8,128)} copy(f32[8,32,256]{2,1,0:T(8,128)} %get-tuple-element.9) | data formatting | bytes 524288

commit v2 on v1

--- a/solution.py
+++ b/solution.py
@@ -73,19 +73,22 @@
 
 def spectral_segment(recv, table, rows, raw, prod, send):
     lane = lax.broadcasted_iota(jnp.int32, (8, 128), 1)
-    totals = [None] * 3
-    for x in range(8):
-        tiles = [recv[(4 * x + r) * 8 : (4 * x + r) * 8 + 8, :] for r in range(4)]
-        got = swap_groups(tiles, lane)
+    totals = [[None] * 3, [None] * 3]
+    for y in range(2):
+        own = slice(8 * y, 8 * y + 8)
+        for x in range(8):
+            tiles = [recv[(4 * x + r) * 16 + 8 * y : (4 * x + r) * 16 + 8 * y + 8, :] for r in range(4)]
+            got = swap_groups(tiles, lane)
+            for c in range(3):
+                raw[c, own, 128 * x : 128 * x + 128] = got[c]
+                totals[y][c] = got[c] if x == 0 else totals[y][c] + got[c]
+    for y in range(2):
+        own = slice(8 * y, 8 * y + 8)
         for c in range(3):
-            raw[c, :, 128 * x : 128 * x + 128] = got[c]
-            totals[c] = got[c] if x == 0 else totals[c] + got[c]
-    for c in range(3):
-        mean = jnp.sum(totals[c], axis=1, keepdims=True) * (1.0 / LENGTH)
-        for j in range(4):
-            rows[j * 24 + c * 8 : j * 24 + c * 8 + 8, :] = (
-                raw[c, :, TILE * j : TILE * j + TILE] - mean
-            )
+            mean = jnp.sum(totals[y][c], axis=1, keepdims=True) * (1.0 / LENGTH)
+            for j in range(4):
+                at = j * 48 + c * 16 + 8 * y
+                rows[at : at + 8, :] = raw[c, own, TILE * j : TILE * j + TILE] - mean
     high, low = split(rows[...])
     both = jnp.concatenate([high, low], axis=0)
     for m in range(8):
@@ -93,34 +96,36 @@
         lows = slice(2 * LENGTH + TILE * m, 2 * LENGTH + TILE * m + TILE)
         main = jnp.dot(both, table[:, cols], preferred_element_type=f32)
         rest = jnp.dot(high, table[:, lows], preferred_element_type=f32)
-        prod[:, cols] = main[:96] + main[96:] + rest
-    segment = [[], [], []]
-    for k in range(4):
-        speed = raw[0, :, TILE * k : TILE * k + TILE]
+        prod[:, cols] = main[:192] + main[192:] + rest
+    within = lane % 32
+    for y in range(2):
+        segment = [[], [], []]
+        for k in range(4):
+            speed = raw[0, 8 * y : 8 * y + 8, TILE * k : TILE * k + TILE]
+            for c in range(3):
+                first = second = None
+                for j in range(4):
+                    m = (k - j) % 4
+                    at = slice(j * 48 + c * 16 + 8 * y, j * 48 + c * 16 + 8 * y + 8)
+                    a = prod[at, TILE * m : TILE * m + TILE]
+                    b = prod[at, LENGTH + TILE * m : LENGTH + TILE * m + TILE]
+                    first = a if j == 0 else first + a
+                    second = b if j == 0 else second + b
+                at = k * 48 + c * 16 + 8 * y
+                value = rows[at : at + 8, :] + (second - speed * first)
+                segment[c] += [value[:, :128], value[:, 128:]]
+        halo = [jnp.zeros((8, 128), f32)] * 8
         for c in range(3):
-            first = second = None
-            for j in range(4):
-                m = (k - j) % 4
-                at = slice(j * 24 + c * 8, j * 24 + c * 8 + 8)
-                a = prod[at, TILE * m : TILE * m + TILE]
-                b = prod[at, LENGTH + TILE * m : LENGTH + TILE * m + TILE]
-                first = a if j == 0 else first + a
-                second = b if j == 0 else second + b
-            own = rows[k * 24 + c * 8 : k * 24 + c * 8 + 8, :]
-            value = own + (second - speed * first)
-            segment[c] += [value[:, :128], value[:, 128:]]
-    within = lane % 32
-    halo = [jnp.zeros((8, 128), f32)] * 8
-    for c in range(3):
-        low_side = shift_lanes(segment[c], 2 + 4 * c)
-        high_side = shift_lanes(segment[c], -30 + 4 * c)
+            low_side = shift_lanes(segment[c], 2 + 4 * c)
+            high_side = shift_lanes(segment[c], -30 + 4 * c)
+            for x in range(8):
+                halo[x] = jnp.where(within // 2 == 2 * c, low_side[x], halo[x])
+                halo[x] = jnp.where(within // 2 == 2 * c + 1, high_side[x], halo[x])
         for x in range(8):
-            halo[x] = jnp.where(within // 2 == 2 * c, low_side[x], halo[x])
-            halo[x] = jnp.where(within // 2 == 2 * c + 1, high_side[x], halo[x])
-    for x in range(8):
-        tiles = swap_groups([segment[0][x], segment[1][x], segment[2][x], halo[x]], lane)
-        for r in range(4):
-            send[(4 * x + r) * 8 : (4 * x + r) * 8 + 8, :] = tiles[r]
+            tiles = swap_groups([segment[0][x], segment[1][x], segment[2][x], halo[x]], lane)
+            for r in range(4):
+                at = (4 * x + r) * 16 + 8 * y
+                send[at : at + 8, :] = tiles[r]
 
 
 def spline_matrix(base, frac, first_cell):
@@ -186,9 +191,9 @@
         slopes[2, z] = advect_rate * slope_z
 
 
-def finish(recv, weights, slopes, still, lhs, seg_out, sc_out):
+def tail(tiles, weights, slopes, still, seg_out, sc_out, lhs):
     for z in range(8):
-        tile = recv[pl.ds(z, 32, stride=8), :]
+        tile = tiles[pl.ds(z, 32, stride=8), :]
         lhs[32 * z : 32 * z + 32, :] = tile
         seg_out[pl.ds(z, 96, stride=8), :] = tile.T[:96]
     high, low = split(lhs[...])
@@ -207,18 +212,23 @@
 
 
 def kernel(
-    vel_in, sc_in, base_in, frac_in, tab_in, seg_out, sc_out,
-    vel, sc, tab, send1, recv1, send2, recv2, rows, raw, prod, lhs,
-    zhalo, ysend, yhalo, ypad, xsend, xhalo, slopes, still,
+    vel_in, sc_in, base_in, frac_in, tab_in, tiles_out, weights_out, slopes, still,
+    vel, sc, tab, base, frac, send1, recv1, send2, recv2, rows, raw, prod,
+    zhalo, ysend, yhalo, ypad, xsend, xhalo,
     load_sem, a_send, a_recv, b_send, b_recv, h_send, h_recv,
 ):
     me = lax.axis_index("blk")
     grp, dep = lax.axis_index("grp"), lax.axis_index("dep")
     n_grp, n_dep = lax.axis_size("grp"), lax.axis_size("dep")
+    owner = lax.rem(me, 2)
+    owns = owner == 1
+    mesh_id = pl.DeviceIdType.MESH
 
     loads = [
         pltpu.make_async_copy(src, dst, load_sem.at[i])
-        for i, (src, dst) in enumerate(((vel_in, vel), (sc_in, sc), (tab_in, tab)))
+        for i, (src, dst) in enumerate(
+            ((vel_in, vel), (sc_in, sc), (tab_in, tab), (base_in, base), (frac_in, frac))
+        )
     ]
     for load in loads:
         load.start()
@@ -232,22 +242,58 @@
         {"blk": lax.rem(me + 1, GROUP)},
         {"blk": lax.rem(me + GROUP - 1, GROUP)},
     )
-
-    def far_first(j):
-        half = (j + 1) // 2
-        offset = 16 + half * (2 * lax.rem(j, 2) - 1)
-        return lax.rem(me + offset, GROUP)
+    z_first, y_first, x_first = lax.rem(dep, 2), 1 - lax.rem(grp, 2), 1 - owner
+
+    def around(j, half):
+        return half + ((j + 1) // 2) * (2 * lax.rem(j, 2) - 1)
+
+    def peer_of(j):
+        return lax.rem(me + around(j, 16), GROUP)
+
+    def owner_of(j):
+        return lax.rem(me // 2 + around(j, 8), 16)
 
     def greet(j, carry):
-        pl.semaphore_signal(barrier, inc=1, device_id={"blk": far_first(j)}, device_id_type=pl.DeviceIdType.MESH)
+        pl.semaphore_signal(barrier, inc=1, device_id={"blk": peer_of(j)}, device_id_type=mesh_id)
         return carry
 
-    lax.fori_loop(0, GROUP - 1, greet, 0)
-    for peer in near[:4]:
-        pl.semaphore_signal(barrier, inc=1, device_id=peer, device_id_type=pl.DeviceIdType.MESH)
+    lax.fori_loop(0, owner * (GROUP - 1), greet, 0)
+    for first, at in ((z_first, 0), (y_first, 2)):
+
+        @pl.when(first == 0)
+        def _():
+            for peer in near[at : at + 2]:
+                pl.semaphore_signal(barrier, inc=1, device_id=peer, device_id_type=mesh_id)
 
     loads[0].wait()
     pack_velocity(vel, send1)
+    pl.semaphore_wait(barrier, 16 - owner + 2 * z_first + 2 * y_first)
+
+    def piece(buffer, index):
+        return buffer.at[pl.ds(pl.multiple_of(index * 16, 16), 16)]
+
+    def to_owner(j, carry):
+        index = owner_of(j)
+        pltpu.make_async_remote_copy(
+            src_ref=piece(send1, index), dst_ref=piece(recv1, me), send_sem=a_send, recv_sem=a_recv,
+            device_id={"blk": 2 * index + 1}, device_id_type=mesh_id,
+        ).start()
+        return carry
+
+    def to_peer(j, carry):
+        peer = peer_of(j)
+        pltpu.make_async_remote_copy(
+            src_ref=piece(send2, peer), dst_ref=piece(recv2, me // 2), send_sem=b_send, recv_sem=b_recv,
+            device_id={"blk": peer}, device_id_type=mesh_id,
+        ).start()
+        return carry
+
+    def settle(buffer, count, sem):
+        part = buffer.at[pl.ds(0, 16 * count)]
+        pltpu.make_async_copy(part, part, sem).wait()
+
+    lax.fori_loop(0, 16 - owner, to_owner, 0)
+
     loads[1].wait()
     for h in range(2):
         ysend[0, :, 4 * h : 4 * h + 4, :] = sc[4 * h : 4 * h + 4, 28:32, :]
@@ -255,31 +301,6 @@
     flat = sc[...].reshape(TILE, TILE)
     xsend[0] = flat[:, 128:].T[120:]
     xsend[1] = flat[:, :128].T[:8]
-    pl.semaphore_wait(barrier, GROUP - 1 + 4)
-
-    def exchange(src, dst, send_sem, recv_sem):
-        def step(j, carry):
-            peer = far_first(j)
-            pltpu.make_async_remote_copy(
-                src_ref=src.at[pl.ds(pl.multiple_of(peer * 8, 8), 8)],
-                dst_ref=dst.at[pl.ds(pl.multiple_of(me * 8, 8), 8)],
-                send_sem=send_sem,
-                recv_sem=recv_sem,
-                device_id={"blk": peer},
-                device_id_type=pl.DeviceIdType.MESH,
-            ).start()
-            return carry
-
-        lax.fori_loop(0, GROUP - 1, step, 0)
-        at = pl.ds(pl.multiple_of(me * 8, 8), 8)
-        dst[at, :] = src[at, :]
-
-    def settle(buffer, sem):
-        part = buffer.at[pl.ds(0, (GROUP - 1) * 8)]
-        pltpu.make_async_copy(part, part, sem).wait()
-
-    exchange(send1, recv1, a_send, a_recv)
-    halos = []
     pieces = (
         (sc.at[pl.ds(4, 4)], zhalo.at[0]),
         (sc.at[pl.ds(0, 4)], zhalo.at[1]),
@@ -288,66 +309,109 @@
         (xsend.at[0], xhalo.at[0]),
         (xsend.at[1], xhalo.at[1]),
     )
-    for i, (src, dst) in enumerate(pieces):
-        copy = pltpu.make_async_remote_copy(
+    halos = [
+        pltpu.make_async_remote_copy(
             src_ref=src, dst_ref=dst, send_sem=h_send.at[i], recv_sem=h_recv.at[i],
-            device_id=near[i], device_id_type=pl.DeviceIdType.MESH,
+            device_id=near[i], device_id_type=mesh_id,
         )
-        copy.start()
-        halos.append(copy)
+        for i, (src, dst) in enumerate(pieces)
+    ]
+    sides = ((x_first, halos[4:6]), (y_first, halos[2:4]), (z_first, halos[0:2]))
+    for first, pair in sides:
+
+        @pl.when(first == 1)
+        def _():
+            for copy in pair:
+                copy.start()
+
     loads[2].wait()
-    settle(recv1, a_recv)
-    spectral_segment(recv1, tab, rows, raw, prod, send2)
-    exchange(send2, recv2, b_send, b_recv)
-
-    weights = spline_matrix(base_in[...], frac_in[...], me * GROUP)
-    for copy in halos:
-        copy.wait()
+
+    @pl.when(owns)
+    def _():
+        recv1[pl.ds(pl.multiple_of(me * 16, 16), 16), :] = send1[pl.ds(pl.multiple_of(me // 2 * 16, 16), 16), :]
+        settle(recv1, GROUP - 1, a_recv)
+        spectral_segment(recv1, tab, rows, raw, prod, send2)
+        lax.fori_loop(0, GROUP - 1, to_peer, 0)
+        recv2[pl.ds(pl.multiple_of(me // 2 * 16, 16), 16), :] = send2[pl.ds(pl.multiple_of(me * 16, 16), 16), :]
+
+    loads[3].wait()
+    loads[4].wait()
+    spline = spline_matrix(base[...], frac[...], me * GROUP)
+    for c in range(3):
+        weights_out[c] = spline[c]
+    for first, pair in sides:
+
+        @pl.when(first == 0)
+        def _():
+            for copy in pair:
+                copy.wait_recv()
+            for copy in pair:
+                copy.start()
+
+    for first, pair in sides:
+
+        @pl.when(first == 1)
+        def _():
+            for copy in pair:
+                copy.wait_recv()
+
     ypad[:, 8:40, :] = sc[...]
     for h in range(2):
         at = slice(4 * h, 4 * h + 4)
         ypad[at, 4:8, :] = yhalo[0, :, at, :]
         ypad[at, 40:44, :] = yhalo[1, :, at, :]
     stencils(sc, zhalo, ypad, xhalo, slopes, still)
-    settle(recv2, b_recv)
-    finish(recv2, weights, slopes, still, lhs, seg_out, sc_out)
-    settle(send1, a_send)
-    settle(send2, b_send)
+
+    @pl.when(owns)
+    def _():
+        settle(recv2, 15, b_recv)
+        settle(send1, 15, a_send)
+        settle(send2, GROUP - 1, b_send)
+
+    @pl.when(jnp.logical_not(owns))
+    def _():
+        settle(recv2, 16, b_recv)
+        settle(send1, 16, a_send)
+
+    tiles_out[...] = recv2[...]
+    for copy in halos:
+        copy.wait_send()
 
 
 def per_device(velocity, scalar, spline_base, spline_frac):
     vmem = pl.BlockSpec(memory_space=pltpu.VMEM)
-    anywhere = pl.BlockSpec(memory_space=pl.ANY)
+    hbm = pl.BlockSpec(memory_space=pltpu.HBM)
     tables = jnp.asarray(spectral_tables())
-    segment, out = pl.pallas_call(
+    parts = pl.pallas_call(
         kernel,
         out_shape=(
-            jax.ShapeDtypeStruct((768, 32), f32),
+            jax.ShapeDtypeStruct((TILE, 128), f32),
+            jax.ShapeDtypeStruct((3, 128, TILE), f32),
+            jax.ShapeDtypeStruct((3, 8, 32, TILE), f32),
             jax.ShapeDtypeStruct((8, 32, TILE), f32),
         ),
-        in_specs=[anywhere, anywhere, vmem, vmem, anywhere],
-        out_specs=(vmem, vmem),
+        in_specs=[hbm] * 5,
+        out_specs=(vmem,) * 4,
         scratch_shapes=[
             pltpu.VMEM((768, 32), f32),
             pltpu.VMEM((8, 32, TILE), f32),
             pltpu.VMEM((TILE, 4 * LENGTH), bf16),
+            pltpu.VMEM((1, TILE), jnp.int32),
+            pltpu.VMEM((1, TILE), f32),
             pltpu.VMEM((TILE, 128), f32),
+            pltpu.VMEM((2 * TILE, 128), f32),
+            pltpu.VMEM((2 * TILE, 128), f32),
             pltpu.VMEM((TILE, 128), f32),
-            pltpu.VMEM((TILE, 128), f32),
-            pltpu.VMEM((TILE, 128), f32),
-            pltpu.VMEM((96, TILE), f32),
-            pltpu.VMEM((3, 8, LENGTH), f32),
-            pltpu.VMEM((96, 2 * LENGTH), f32),
-            pltpu.VMEM((TILE, 128), f32),
+            pltpu.VMEM((192, TILE), f32),
+            pltpu.VMEM((3, 16, LENGTH), f32),
+            pltpu.VMEM((192, 2 * LENGTH), f32),
             pltpu.VMEM((2, 4, 32, TILE), f32),
             pltpu.VMEM((2, 4, 8, TILE), f32),
             pltpu.VMEM((2, 4, 8, TILE), f32),
             pltpu.VMEM((8, 48, TILE), f32),
             pltpu.VMEM((2, 8, TILE), f32),
             pltpu.VMEM((2, 8, TILE), f32),
-            pltpu.VMEM((3, 8, 32, TILE), f32),
-            pltpu.VMEM((8, 32, TILE), f32),
-            pltpu.SemaphoreType.DMA((3,)),
+            pltpu.SemaphoreType.DMA((5,)),
             pltpu.SemaphoreType.DMA,
             pltpu.SemaphoreType.DMA,
             pltpu.SemaphoreType.DMA,
@@ -355,15 +419,34 @@
             pltpu.SemaphoreType.DMA((6,)),
             pltpu.SemaphoreType.DMA((6,)),
         ],
-        compiler_params=pltpu.CompilerParams(collective_id=0, has_side_effects=True),
+        compiler_params=pltpu.CompilerParams(
+            collective_id=0, has_side_effects=True, vmem_limit_bytes=24 * 2**20
+        ),
         name="segment",
     )(
-        velocity.reshape(768, 32),
-        scalar,
-        spline_base.reshape(1, TILE),
-        spline_frac.reshape(1, TILE),
-        tables,
+        *(
+            pltpu.with_memory_space_constraint(x, pltpu.HBM)
+            for x in (
+                velocity.reshape(768, 32),
+                scalar,
+                spline_base.reshape(1, TILE),
+                spline_frac.reshape(1, TILE),
+                tables,
+            )
+        )
     )
+    segment, out = pl.pallas_call(
+        tail,
+        out_shape=(
+            jax.ShapeDtypeStruct((768, 32), f32),
+            jax.ShapeDtypeStruct((8, 32, TILE), f32),
+        ),
+        in_specs=[vmem] * 4,
+        out_specs=(vmem, vmem),
+        scratch_shapes=[pltpu.VMEM((TILE, 128), f32)],
+        compiler_params=pltpu.CompilerParams(vmem_limit_bytes=24 * 2**20),
+        name="tail",
+    )(*parts)
     return segment.reshape(velocity.shape), out
 
 

time: 38.6 us -> 31.6 us (0.82)
  the two profiles are of different devices: /device:TPU:1 before, /device:TPU:128 now
where the time goes in v2:
time: 31.6 us; the launch traced here: 31.4 us
  Pallas kernels  30.8 us (97%)
  between operations  0.64 us (2%)
    pallas_call x1, Pallas kernels, per_device(): pl.pallas_call(kernel, out_shape=(jax.ShapeDtypeStruct((TILE, 128), f32),...  29.6 us
    pallas_call x1, Pallas kernels, per_device(): pl.pallas_call(tail, out_shape=(jax.ShapeDtypeStruct((768, 32), f32), jax...  1.17 us

profile of v2, /device:TPU:128, one launch (start us, length us, event | category | flops | bytes accessed | tf_op | source)
XLA Modules:
  0.0 31.4 jit_solution(1426521107062594258)
XLA Ops:
  0.6 29.6 %segment.1 = (f32[256,128]{1,0:T(8,128)S(1)}, f32[3,128,256]{2,1,0:T(8,128)S(1)}, f32[3,8,32,256]{3,2,1,0:T(8,128)S(1)}, f32[8,32,256]{2,1,0:T(8,128)S(1)}) custom-call(f32[768,32]{1,0:T(8,128)} %bitcast.4, f32[8,32,256]{2,1,0:T(8,128)} %sc_in.1, s32[1,256]{1,0:T(1,128)} %bitcast.5, f32[1,256]{1,0:T(1,128)} %bitcast.6, bf16[256,4096]{1,0:T(8,128)(2,1)} %constant.2.clone.tab_in), custom_call_target="tpu_custom_call" | custom-call | tf_op jit(solution)/shard_map/segment/pallas_call | solution.py:385
  30.2 1.2 %tail.1 = (f32[768,32]{1,0:T(8,128)}, f32[8,32,256]{2,1,0:T(8,128)}) custom-call(f32[256,128]{1,0:T(8,128)S(1)} %get-tuple-element.8.tiles, f32[3,128,256]{2,1,0:T(8,128)S(1)} %get-tuple-element.9.weights, f32[3,8,32,256]{3,2,1,0:T(8,128)S(1)} %get-tuple-element.10.slopes, f32[8,32,256]{2,1,0:T(8,128)S(1)} %get-tuple-element.11.still), custom_call_target="tpu_custom_call" | custom-call | tf_op jit(solution)/shard_map/tail/pallas_call | solution.py:438

commit v3 on v2

--- a/solution.py
+++ b/solution.py
@@ -160,34 +160,40 @@
     return slope, curve
 
 
-def stencils(sc, zhalo, ypad, xhalo, slopes, still):
+def stencils_xy(sc, ypad, xhalo, slopes, still):
     pad = jnp.zeros((120, TILE), f32)
     left = jnp.concatenate([pad, xhalo[0]], axis=0).T
     right = jnp.concatenate([xhalo[1], pad], axis=0).T
     for z in range(8):
         own = sc[z]
 
+        def along_y(m):
+            return ypad[z, 8 + m : 40 + m, :]
+
+        wide = jnp.concatenate([left[32 * z : 32 * z + 32], own, right[32 * z : 32 * z + 32]], axis=1)
+
+        def along_x(m):
+            return pltpu.roll(wide, (-m) % 512, axis=1)[:, 128:384]
+
+        slope_y, curve_y = pair_sums(along_y)
+        slope_x, curve_x = pair_sums(along_x)
+        curve = curve_y + curve_x + (3.0 * second_centre) * own
+        still[z] = own + diffuse_rate * curve
+        slopes[0, z] = advect_rate * slope_x
+        slopes[1, z] = advect_rate * slope_y
+
+
+def stencils_z(sc, zhalo, slopes, still):
+    for z in range(8):
+
         def along_z(m):
             at = z + m
             if at < 0:
                 return zhalo[0, 4 + at]
             return zhalo[1, at - 8] if at >= 8 else sc[at]
 
-        def along_y(m):
-            return ypad[z, 8 + m : 40 + m, :]
-
-        wide = jnp.concatenate([left[32 * z : 32 * z + 32], own, right[32 * z : 32 * z + 32]], axis=1)
-
-        def along_x(m):
-            return pltpu.roll(wide, (-m) % 512, axis=1)[:, 128:384]
-
         slope_z, curve_z = pair_sums(along_z)
-        slope_y, curve_y = pair_sums(along_y)
-        slope_x, curve_x = pair_sums(along_x)
-        curve = curve_z + curve_y + curve_x + (3.0 * second_centre) * own
-        still[z] = own + diffuse_rate * curve
-        slopes[0, z] = advect_rate * slope_x
-        slopes[1, z] = advect_rate * slope_y
+        still[z] = still[z] + diffuse_rate * curve_z
         slopes[2, z] = advect_rate * slope_z
 
 
@@ -215,14 +221,31 @@
     vel_in, sc_in, base_in, frac_in, tab_in, tiles_out, weights_out, slopes, still,
     vel, sc, tab, base, frac, send1, recv1, send2, recv2, rows, raw, prod,
     zhalo, ysend, yhalo, ypad, xsend, xhalo,
-    load_sem, a_send, a_recv, b_send, b_recv, h_send, h_recv,
+    load_sem, a_send, a_recv, b_send, b_recv, h_send, h_recv, hello, go, met,
 ):
     me = lax.axis_index("blk")
     grp, dep = lax.axis_index("grp"), lax.axis_index("dep")
     n_grp, n_dep = lax.axis_size("grp"), lax.axis_size("dep")
-    owner = lax.rem(me, 2)
-    owns = owner == 1
     mesh_id = pl.DeviceIdType.MESH
+    x, rest = me // 4, lax.rem(me, 4)
+    owner = x // 6 + lax.rem((x + 1) // 2, 2) * (1 - x // 4)
+    owns, guest = owner == 1, owner == 0
+    mine = (x - 1 - 3 * (x // 6)) * 4 + rest
+    host = ((x // 3) * (1 - x // 4) + (x - 2) * (x // 4)) * 4 + rest
+
+    def owner_at(index):
+        return (index // 4 + 1 + 3 * (index // 8)) * 4 + lax.rem(index, 4)
+
+    def cube(bit):
+        size = 2**bit
+        return {"blk": owner_at(mine + size * (1 - 2 * lax.rem(mine // size, 2)))}
+
+    def guest_at():
+        q = mine // 4
+        return {"blk": (3 * q * (1 - q // 2) + (q + 2) * (q // 2)) * 4 + rest}
+
+    def signal(sem, peer):
+        pl.semaphore_signal(sem, inc=1, device_id=peer, device_id_type=mesh_id)
 
     loads = [
         pltpu.make_async_copy(src, dst, load_sem.at[i])
@@ -230,8 +253,8 @@
             ((vel_in, vel), (sc_in, sc), (tab_in, tab), (base_in, base), (frac_in, frac))
         )
     ]
-    for load in loads:
-        load.start()
+    for i in (0, 1, 3, 4):
+        loads[i].start()
 
     barrier = pltpu.get_barrier_semaphore()
     near = (
@@ -242,68 +265,36 @@
         {"blk": lax.rem(me + 1, GROUP)},
         {"blk": lax.rem(me + GROUP - 1, GROUP)},
     )
-    z_first, y_first, x_first = lax.rem(dep, 2), 1 - lax.rem(grp, 2), 1 - owner
-
-    def around(j, half):
-        return half + ((j + 1) // 2) * (2 * lax.rem(j, 2) - 1)
-
-    def peer_of(j):
-        return lax.rem(me + around(j, 16), GROUP)
-
-    def owner_of(j):
-        return lax.rem(me // 2 + around(j, 8), 16)
+    up, down = dep // (n_dep - 1), (dep + n_dep - 1) // n_dep
+    high, middle = grp // 2, lax.rem((grp + 1) // 2, 2)
+    turned = (dep + n_dep - 1) // n_dep
+    ahead = 1 - lax.rem(me, 2) + turned * (me // (GROUP - 1))
+    behind = 1 - lax.rem(me, 2) - turned * ((GROUP - me) // GROUP)
+    first = (up, down, high, middle, ahead, behind)
+    for i in range(6):
+
+        @pl.when(first[i] == 0)
+        def _():
+            signal(barrier, near[i])
 
     def greet(j, carry):
-        pl.semaphore_signal(barrier, inc=1, device_id={"blk": peer_of(j)}, device_id_type=mesh_id)
+        signal(barrier, {"blk": j + (j - me + GROUP) // GROUP})
         return carry
 
-    lax.fori_loop(0, owner * (GROUP - 1), greet, 0)
-    for first, at in ((z_first, 0), (y_first, 2)):
-
-        @pl.when(first == 0)
-        def _():
-            for peer in near[at : at + 2]:
-                pl.semaphore_signal(barrier, inc=1, device_id=peer, device_id_type=mesh_id)
-
-    loads[0].wait()
-    pack_velocity(vel, send1)
-    pl.semaphore_wait(barrier, 16 - owner + 2 * z_first + 2 * y_first)
-
-    def piece(buffer, index):
-        return buffer.at[pl.ds(pl.multiple_of(index * 16, 16), 16)]
-
-    def to_owner(j, carry):
-        index = owner_of(j)
-        pltpu.make_async_remote_copy(
-            src_ref=piece(send1, index), dst_ref=piece(recv1, me), send_sem=a_send, recv_sem=a_recv,
-            device_id={"blk": 2 * index + 1}, device_id_type=mesh_id,
-        ).start()
-        return carry
-
-    def to_peer(j, carry):
-        peer = peer_of(j)
-        pltpu.make_async_remote_copy(
-            src_ref=piece(send2, peer), dst_ref=piece(recv2, me // 2), send_sem=b_send, recv_sem=b_recv,
-            device_id={"blk": peer}, device_id_type=mesh_id,
-        ).start()
-        return carry
-
-    def settle(buffer, count, sem):
-        part = buffer.at[pl.ds(0, 16 * count)]
-        pltpu.make_async_copy(part, part, sem).wait()
-
-    lax.fori_loop(0, 16 - owner, to_owner, 0)
-
-    loads[1].wait()
-    for h in range(2):
-        ysend[0, :, 4 * h : 4 * h + 4, :] = sc[4 * h : 4 * h + 4, 28:32, :]
-        ysend[1, :, 4 * h : 4 * h + 4, :] = sc[4 * h : 4 * h + 4, 0:4, :]
-    flat = sc[...].reshape(TILE, TILE)
-    xsend[0] = flat[:, 128:].T[120:]
-    xsend[1] = flat[:, :128].T[:8]
+    lax.fori_loop(0, owner * (1 - up) * (GROUP - 1), greet, 0)
+
+    @pl.when(owner * up == 1)
+    def _():
+        signal(barrier, guest_at())
+        for bit in range(4):
+            signal(barrier, cube(bit))
+
+    expected = (1 - up) * (16 - owner) + up * (1 + 3 * owner)
+    pl.semaphore_wait(barrier, expected + up + down + high + middle + ahead + behind)
+
     pieces = (
-        (sc.at[pl.ds(4, 4)], zhalo.at[0]),
-        (sc.at[pl.ds(0, 4)], zhalo.at[1]),
+        (sc_in.at[pl.ds(4, 4)], zhalo.at[0]),
+        (sc_in.at[pl.ds(0, 4)], zhalo.at[1]),
         (ysend.at[0], yhalo.at[0]),
         (ysend.at[1], yhalo.at[1]),
         (xsend.at[0], xhalo.at[0]),
@@ -316,51 +307,124 @@
         )
         for i, (src, dst) in enumerate(pieces)
     ]
-    sides = ((x_first, halos[4:6]), (y_first, halos[2:4]), (z_first, halos[0:2]))
-    for first, pair in sides:
-
-        @pl.when(first == 1)
-        def _():
-            for copy in pair:
-                copy.start()
-
-    loads[2].wait()
+
+    def send_first(indices):
+        for i in indices:
+
+            @pl.when(first[i] == 1)
+            def _():
+                halos[i].start()
+
+    def reply(indices):
+        for i in indices:
+
+            @pl.when(first[i] == 0)
+            def _():
+                halos[i ^ 1].wait_recv()
+                halos[i].start()
+
+    def receive(indices):
+        for i in indices:
+
+            @pl.when(first[i] == 1)
+            def _():
+                halos[i ^ 1].wait_recv()
+
+    def piece(buffer, index):
+        return buffer.at[pl.ds(pl.multiple_of(index * 16, 16), 16)]
+
+    def to_owner(start):
+        def step(j, carry):
+            index = lax.rem(start + j, 16)
+            pltpu.make_async_remote_copy(
+                src_ref=piece(send1, index), dst_ref=piece(recv1, me), send_sem=a_send, recv_sem=a_recv,
+                device_id={"blk": owner_at(index)}, device_id_type=mesh_id,
+            ).start()
+            return carry
+
+        return step
+
+    def to_peer(j, carry):
+        peer = j + (j - me + GROUP) // GROUP
+        pltpu.make_async_remote_copy(
+            src_ref=piece(send2, peer), dst_ref=piece(recv2, mine), send_sem=b_send, recv_sem=b_recv,
+            device_id={"blk": peer}, device_id_type=mesh_id,
+        ).start()
+        return carry
+
+    def settle(buffer, count, sem):
+        part = buffer.at[pl.ds(0, 16 * count)]
+        pltpu.make_async_copy(part, part, sem).wait()
+
+    @pl.when((1 - owner) * up == 1)
+    def _():
+        signal(hello, {"blk": owner_at(host)})
+
+    @pl.when(owner * up == 1)
+    def _():
+        signal(met.at[0], cube(0))
+
+    send_first((0, 1))
+    loads[0].wait()
+    pack_velocity(vel, send1)
+
+    @pl.when((1 - owner) * up == 1)
+    def _():
+        pl.semaphore_wait(go, 1)
+
+    @pl.when(owner * up == 1)
+    def _():
+        for bit in range(4):
+            pl.semaphore_wait(met.at[bit], 1)
+            if bit < 3:
+                signal(met.at[bit + 1], cube(bit + 1))
+
+    lax.fori_loop(0, 16 - owner, to_owner(owner * (mine + 1) + 4 * (1 - owner)), 0)
+
+    @pl.when(owner * up == 1)
+    def _():
+        pl.semaphore_wait(hello, 1)
+        signal(go, guest_at())
 
     @pl.when(owns)
     def _():
-        recv1[pl.ds(pl.multiple_of(me * 16, 16), 16), :] = send1[pl.ds(pl.multiple_of(me // 2 * 16, 16), 16), :]
+        loads[2].start()
+
+    loads[1].wait()
+    for h in range(2):
+        ysend[0, :, 4 * h : 4 * h + 4, :] = sc[4 * h : 4 * h + 4, 28:32, :]
+        ysend[1, :, 4 * h : 4 * h + 4, :] = sc[4 * h : 4 * h + 4, 0:4, :]
+    flat = sc[...].reshape(TILE, TILE)
+    xsend[0] = flat[:, 128:].T[120:]
+    xsend[1] = flat[:, :128].T[:8]
+    send_first((4, 5, 2, 3))
+    reply((4, 5))
+
+    @pl.when(owns)
+    def _():
+        loads[2].wait()
+        recv1[pl.ds(pl.multiple_of(me * 16, 16), 16), :] = send1[pl.ds(pl.multiple_of(mine * 16, 16), 16), :]
         settle(recv1, GROUP - 1, a_recv)
         spectral_segment(recv1, tab, rows, raw, prod, send2)
         lax.fori_loop(0, GROUP - 1, to_peer, 0)
-        recv2[pl.ds(pl.multiple_of(me // 2 * 16, 16), 16), :] = send2[pl.ds(pl.multiple_of(me * 16, 16), 16), :]
-
+        recv2[pl.ds(pl.multiple_of(mine * 16, 16), 16), :] = send2[pl.ds(pl.multiple_of(me * 16, 16), 16), :]
+
+    reply((2, 3, 0))
     loads[3].wait()
     loads[4].wait()
     spline = spline_matrix(base[...], frac[...], me * GROUP)
     for c in range(3):
         weights_out[c] = spline[c]
-    for first, pair in sides:
-
-        @pl.when(first == 0)
-        def _():
-            for copy in pair:
-                copy.wait_recv()
-            for copy in pair:
-                copy.start()
-
-    for first, pair in sides:
-
-        @pl.when(first == 1)
-        def _():
-            for copy in pair:
-                copy.wait_recv()
-
+    receive((4, 5, 2, 3))
     ypad[:, 8:40, :] = sc[...]
     for h in range(2):
         at = slice(4 * h, 4 * h + 4)
         ypad[at, 4:8, :] = yhalo[0, :, at, :]
         ypad[at, 40:44, :] = yhalo[1, :, at, :]
-    stencils(sc, zhalo, ypad, xhalo, slopes, still)
+    stencils_xy(sc, ypad, xhalo, slopes, still)
+    reply((1,))
+    receive((0, 1))
+    stencils_z(sc, zhalo, slopes, still)
 
     @pl.when(owns)
     def _():
@@ -368,7 +432,7 @@
         settle(send1, 15, a_send)
         settle(send2, GROUP - 1, b_send)
 
-    @pl.when(jnp.logical_not(owns))
+    @pl.when(guest)
     def _():
         settle(recv2, 16, b_recv)
         settle(send1, 16, a_send)
@@ -418,6 +482,9 @@
             pltpu.SemaphoreType.DMA,
             pltpu.SemaphoreType.DMA((6,)),
             pltpu.SemaphoreType.DMA((6,)),
+            pltpu.SemaphoreType.REGULAR,
+            pltpu.SemaphoreType.REGULAR,
+            pltpu.SemaphoreType.REGULAR((4,)),
         ],
         compiler_params=pltpu.CompilerParams(
             collective_id=0, has_side_effects=True, vmem_limit_bytes=24 * 2**20

time: 31.6 us -> 29.7 us (0.940)
  the two profiles are of different devices: /device:TPU:128 before, /device:TPU:5 now
where the time goes in v3:
time: 29.7 us; the launch traced here: 29.5 us
  Pallas kernels  28.9 us (97%)
  between operations  0.64 us (2%)
    pallas_call x1, Pallas kernels, per_device(): pl.pallas_call(kernel, out_shape=(jax.ShapeDtypeStruct((TILE, 128), f32),...  27.7 us
    pallas_call x1, Pallas kernels, per_device(): pl.pallas_call(tail, out_shape=(jax.ShapeDtypeStruct((768, 32), f32), jax...  1.17 us

profile of v3, /device:TPU:5, one launch (start us, length us, event | category | flops | bytes accessed | tf_op | source)
XLA Modules:
  0.0 29.5 jit_solution(16232536209667786977)
XLA Ops:
  0.6 27.7 %segment.1 = (f32[256,128]{1,0:T(8,128)S(1)}, f32[3,128,256]{2,1,0:T(8,128)S(1)}, f32[3,8,32,256]{3,2,1,0:T(8,128)S(1)}, f32[8,32,256]{2,1,0:T(8,128)S(1)}) custom-call(f32[768,32]{1,0:T(8,128)} %bitcast.4, f32[8,32,256]{2,1,0:T(8,128)} %sc_in.1, s32[1,256]{1,0:T(1,128)} %bitcast.5, f32[1,256]{1,0:T(1,128)} %bitcast.6, bf16[256,4096]{1,0:T(8,128)(2,1)} %constant.2.clone.tab_in), custom_call_target="tpu_custom_call" | custom-call | tf_op jit(solution)/shard_map/segment/pallas_call | solution.py:449
  28.4 1.2 %tail.1 = (f32[768,32]{1,0:T(8,128)}, f32[8,32,256]{2,1,0:T(8,128)}) custom-call(f32[256,128]{1,0:T(8,128)S(1)} %get-tuple-element.8.tiles, f32[3,128,256]{2,1,0:T(8,128)S(1)} %get-tuple-element.9.weights, f32[3,8,32,256]{3,2,1,0:T(8,128)S(1)} %get-tuple-element.10.slopes, f32[8,32,256]{2,1,0:T(8,128)S(1)} %get-tuple-element.11.still), custom_call_target="tpu_custom_call" | custom-call | tf_op jit(solution)/shard_map/tail/pallas_call | solution.py:505

commit v4 on v3

--- a/solution.py
+++ b/solution.py
@@ -71,7 +71,7 @@
         send[pl.ds(z, 32, stride=8), :] = part.T
 
 
-def spectral_segment(recv, table, rows, raw, prod, send):
+def spectral_segment(recv, table, rows, raw, prod, send, dispatch):
     lane = lax.broadcasted_iota(jnp.int32, (8, 128), 1)
     totals = [[None] * 3, [None] * 3]
     for y in range(2):
@@ -98,6 +98,7 @@
         rest = jnp.dot(high, table[:, lows], preferred_element_type=f32)
         prod[:, cols] = main[:192] + main[192:] + rest
     within = lane % 32
+    packed = []
     for y in range(2):
         segment = [[], [], []]
         for k in range(4):
@@ -121,11 +122,16 @@
             for x in range(8):
                 halo[x] = jnp.where(within // 2 == 2 * c, low_side[x], halo[x])
                 halo[x] = jnp.where(within // 2 == 2 * c + 1, high_side[x], halo[x])
-        for x in range(8):
-            tiles = swap_groups([segment[0][x], segment[1][x], segment[2][x], halo[x]], lane)
+        packed.append(segment + [halo])
+    for x in range(8):
+        for y in range(2):
+            tiles = swap_groups([packed[y][c][x] for c in range(4)], lane)
             for r in range(4):
                 at = (4 * x + r) * 16 + 8 * y
                 send[at : at + 8, :] = tiles[r]
+        if x > 0:
+            dispatch(x - 1)
+    dispatch(7)
 
 
 def spline_matrix(base, frac, first_cell):
@@ -197,13 +203,15 @@
         slopes[2, z] = advect_rate * slope_z
 
 
-def tail(tiles, weights, slopes, still, seg_out, sc_out, lhs):
+def tail(tiles, weights, slopes, still, seg_out, sc_out, lhs, seg, sc, sems):
     for z in range(8):
         tile = tiles[pl.ds(z, 32, stride=8), :]
         lhs[32 * z : 32 * z + 32, :] = tile
-        seg_out[pl.ds(z, 96, stride=8), :] = tile.T[:96]
+        seg[pl.ds(z, 96, stride=8), :] = tile.T[:96]
     high, low = split(lhs[...])
     both = jnp.concatenate([high, low], axis=1)
+    copies = [pltpu.make_async_copy(seg, seg_out, sems.at[0])]
+    copies[0].start()
     fine = []
     for c in range(3):
         w_high, w_low = split(weights[c])
@@ -214,7 +222,13 @@
     for z in range(8):
         at = slice(32 * z, 32 * z + 32)
         moved = fine[0][at] * slopes[0, z] + fine[1][at] * slopes[1, z] + fine[2][at] * slopes[2, z]
-        sc_out[z] = still[z] - moved
+        sc[z] = still[z] - moved
+        if z % 4 == 3:
+            half = pl.ds(z - 3, 4)
+            copies.append(pltpu.make_async_copy(sc.at[half], sc_out.at[half], sems.at[1 + z // 4]))
+            copies[-1].start()
+    for copy in copies:
+        copy.wait()
 
 
 def kernel(
@@ -228,21 +242,22 @@
     n_grp, n_dep = lax.axis_size("grp"), lax.axis_size("dep")
     mesh_id = pl.DeviceIdType.MESH
     x, rest = me // 4, lax.rem(me, 4)
-    owner = x // 6 + lax.rem((x + 1) // 2, 2) * (1 - x // 4)
+    owner = lax.rem(x, 2)
     owns, guest = owner == 1, owner == 0
-    mine = (x - 1 - 3 * (x // 6)) * 4 + rest
-    host = ((x // 3) * (1 - x // 4) + (x - 2) * (x // 4)) * 4 + rest
+    mine = x // 2 * 4 + rest
+    host = x // 2 * 4 + rest
 
     def owner_at(index):
-        return (index // 4 + 1 + 3 * (index // 8)) * 4 + lax.rem(index, 4)
+        return (index // 4 * 2 + 1) * 4 + lax.rem(index, 4)
 
     def cube(bit):
+        if bit == 3:
+            return {"blk": owner_at(mine + 4 * (3 - 2 * (mine // 4)))}
         size = 2**bit
         return {"blk": owner_at(mine + size * (1 - 2 * lax.rem(mine // size, 2)))}
 
     def guest_at():
-        q = mine // 4
-        return {"blk": (3 * q * (1 - q // 2) + (q + 2) * (q // 2)) * 4 + rest}
+        return {"blk": me - 4}
 
     def signal(sem, peer):
         pl.semaphore_signal(sem, inc=1, device_id=peer, device_id_type=mesh_id)
@@ -331,7 +346,8 @@
                 halos[i ^ 1].wait_recv()
 
     def piece(buffer, index):
-        return buffer.at[pl.ds(pl.multiple_of(index * 16, 16), 16)]
+        start = index * 16 if isinstance(index, int) else pl.multiple_of(index * 16, 16)
+        return buffer.at[pl.ds(start, 16)]
 
     def to_owner(start):
         def step(j, carry):
@@ -344,13 +360,16 @@
 
         return step
 
-    def to_peer(j, carry):
-        peer = j + (j - me + GROUP) // GROUP
-        pltpu.make_async_remote_copy(
-            src_ref=piece(send2, peer), dst_ref=piece(recv2, mine), send_sem=b_send, recv_sem=b_recv,
-            device_id={"blk": peer}, device_id_type=mesh_id,
-        ).start()
-        return carry
+    def to_column(column):
+        for r in range(4):
+            peer = 4 * column + r
+
+            @pl.when(me != peer)
+            def _():
+                pltpu.make_async_remote_copy(
+                    src_ref=piece(send2, peer), dst_ref=piece(recv2, mine), send_sem=b_send, recv_sem=b_recv,
+                    device_id={"blk": peer}, device_id_type=mesh_id,
+                ).start()
 
     def settle(buffer, count, sem):
         part = buffer.at[pl.ds(0, 16 * count)]
@@ -405,8 +424,7 @@
         loads[2].wait()
         recv1[pl.ds(pl.multiple_of(me * 16, 16), 16), :] = send1[pl.ds(pl.multiple_of(mine * 16, 16), 16), :]
         settle(recv1, GROUP - 1, a_recv)
-        spectral_segment(recv1, tab, rows, raw, prod, send2)
-        lax.fori_loop(0, GROUP - 1, to_peer, 0)
+        spectral_segment(recv1, tab, rows, raw, prod, send2, to_column)
         recv2[pl.ds(pl.multiple_of(mine * 16, 16), 16), :] = send2[pl.ds(pl.multiple_of(me * 16, 16), 16), :]
 
     reply((2, 3, 0))
@@ -509,8 +527,13 @@
             jax.ShapeDtypeStruct((8, 32, TILE), f32),
         ),
         in_specs=[vmem] * 4,
-        out_specs=(vmem, vmem),
-        scratch_shapes=[pltpu.VMEM((TILE, 128), f32)],
+        out_specs=(hbm, hbm),
+        scratch_shapes=[
+            pltpu.VMEM((TILE, 128), f32),
+            pltpu.VMEM((768, 32), f32),
+            pltpu.VMEM((8, 32, TILE), f32),
+            pltpu.SemaphoreType.DMA((3,)),
+        ],
         compiler_params=pltpu.CompilerParams(vmem_limit_bytes=24 * 2**20),
         name="tail",
     )(*parts)

time: 29.7 us -> 28.7 us (0.966)
  the two profiles are of different devices: /device:TPU:5 before, /device:TPU:1 now
where the time goes in v4:
time: 28.7 us; the launch traced here: 28.4 us
  Pallas kernels  27.8 us (97%)
  between operations  0.64 us (2%)
    pallas_call x1, Pallas kernels, per_device(): pl.pallas_call(kernel, out_shape=(jax.ShapeDtypeStruct((TILE, 128), f32),...  26.6 us
    pallas_call x1, Pallas kernels, per_device(): pl.pallas_call(tail, out_shape=(jax.ShapeDtypeStruct((768, 32), f32), jax...  1.15 us

profile of v4, /device:TPU:1, one launch (start us, length us, event | category | flops | bytes accessed | tf_op | source)
XLA Modules:
  0.0 28.4 jit_solution(10746730536794883660)
XLA Ops:
  0.6 26.6 %segment.1 = (f32[256,128]{1,0:T(8,128)S(1)}, f32[3,128,256]{2,1,0:T(8,128)S(1)}, f32[3,8,32,256]{3,2,1,0:T(8,128)S(1)}, f32[8,32,256]{2,1,0:T(8,128)S(1)}) custom-call(f32[768,32]{1,0:T(8,128)} %bitcast.4, f32[8,32,256]{2,1,0:T(8,128)} %sc_in.1, s32[1,256]{1,0:T(1,128)} %bitcast.5, f32[1,256]{1,0:T(1,128)} %bitcast.6, bf16[256,4096]{1,0:T(8,128)(2,1)} %constant.2.clone.tab_in), custom_call_target="tpu_custom_call" | custom-call | tf_op jit(solution)/shard_map/segment/pallas_call | solution.py:467
  27.3 1.2 %tail.1 = (f32[768,32]{1,0:T(8,128)}, f32[8,32,256]{2,1,0:T(8,128)}) custom-call(f32[256,128]{1,0:T(8,128)S(1)} %get-tuple-element.8.tiles, f32[3,128,256]{2,1,0:T(8,128)S(1)} %get-tuple-element.9.weights, f32[3,8,32,256]{3,2,1,0:T(8,128)S(1)} %get-tuple-element.10.slopes, f32[8,32,256]{2,1,0:T(8,128)S(1)} %get-tuple-element.11.still), custom_call_target="tpu_custom_call" | custom-call | tf_op jit(solution)/shard_map/tail/pallas_call | solution.py:523

commit v5 on v4

--- a/solution.py
+++ b/solution.py
@@ -123,15 +123,16 @@
                 halo[x] = jnp.where(within // 2 == 2 * c, low_side[x], halo[x])
                 halo[x] = jnp.where(within // 2 == 2 * c + 1, high_side[x], halo[x])
         packed.append(segment + [halo])
-    for x in range(8):
+    order = (0, 1, 7, 2, 6, 3, 5, 4)
+    for i, x in enumerate(order):
         for y in range(2):
             tiles = swap_groups([packed[y][c][x] for c in range(4)], lane)
             for r in range(4):
                 at = (4 * x + r) * 16 + 8 * y
                 send[at : at + 8, :] = tiles[r]
-        if x > 0:
-            dispatch(x - 1)
-    dispatch(7)
+        if i > 0:
+            dispatch(order[i - 1])
+    dispatch(order[-1])
 
 
 def spline_matrix(base, frac, first_cell):
@@ -268,8 +269,7 @@
             ((vel_in, vel), (sc_in, sc), (tab_in, tab), (base_in, base), (frac_in, frac))
         )
     ]
-    for i in (0, 1, 3, 4):
-        loads[i].start()
+    loads[0].start()
 
     barrier = pltpu.get_barrier_semaphore()
     near = (
@@ -385,6 +385,8 @@
 
     send_first((0, 1))
     loads[0].wait()
+    for i in (1, 3, 4):
+        loads[i].start()
     pack_velocity(vel, send1)
 
     @pl.when((1 - owner) * up == 1)

time: 28.7 us -> 28.6 us (level)
  no operation moved by 1% of the time
where the time goes in v5:
time: 28.6 us; the launch traced here: 28.4 us
  Pallas kernels  27.8 us (97%)
  between operations  0.64 us (2%)
    pallas_call x1, Pallas kernels, per_device(): pl.pallas_call(kernel, out_shape=(jax.ShapeDtypeStruct((TILE, 128), f32),...  26.6 us
    pallas_call x1, Pallas kernels, per_device(): pl.pallas_call(tail, out_shape=(jax.ShapeDtypeStruct((768, 32), f32), jax...  1.15 us

profile of v5, /device:TPU:1, one launch (start us, length us, event | category | flops | bytes accessed | tf_op | source)
XLA Modules:
  0.0 28.4 jit_solution(1035175671692026449)
XLA Ops:
  0.6 26.6 %segment.1 = (f32[256,128]{1,0:T(8,128)S(1)}, f32[3,128,256]{2,1,0:T(8,128)S(1)}, f32[3,8,32,256]{3,2,1,0:T(8,128)S(1)}, f32[8,32,256]{2,1,0:T(8,128)S(1)}) custom-call(f32[768,32]{1,0:T(8,128)} %bitcast.4, f32[8,32,256]{2,1,0:T(8,128)} %sc_in.1, s32[1,256]{1,0:T(1,128)} %bitcast.5, f32[1,256]{1,0:T(1,128)} %bitcast.6, bf16[256,4096]{1,0:T(8,128)(2,1)} %constant.2.clone.tab_in), custom_call_target="tpu_custom_call" | custom-call | tf_op jit(solution)/shard_map/segment/pallas_call | solution.py:469
  27.3 1.1 %tail.1 = (f32[768,32]{1,0:T(8,128)}, f32[8,32,256]{2,1,0:T(8,128)}) custom-call(f32[256,128]{1,0:T(8,128)S(1)} %get-tuple-element.8.tiles, f32[3,128,256]{2,1,0:T(8,128)S(1)} %get-tuple-element.9.weights, f32[3,8,32,256]{3,2,1,0:T(8,128)S(1)} %get-tuple-element.10.slopes, f32[8,32,256]{2,1,0:T(8,128)S(1)} %get-tuple-element.11.still), custom_call_target="tpu_custom_call" | custom-call | tf_op jit(solution)/shard_map/tail/pallas_call | solution.py:525

commit v6 on v5

--- a/solution.py
+++ b/solution.py
@@ -249,7 +249,7 @@
     host = x // 2 * 4 + rest
 
     def owner_at(index):
-        return (index // 4 * 2 + 1) * 4 + lax.rem(index, 4)
+        return (index // 4 * 2 + 1) * 4 + index % 4
 
     def cube(bit):
         if bit == 3:
@@ -349,16 +349,15 @@
         start = index * 16 if isinstance(index, int) else pl.multiple_of(index * 16, 16)
         return buffer.at[pl.ds(start, 16)]
 
-    def to_owner(start):
-        def step(j, carry):
-            index = lax.rem(start + j, 16)
-            pltpu.make_async_remote_copy(
-                src_ref=piece(send1, index), dst_ref=piece(recv1, me), send_sem=a_send, recv_sem=a_recv,
-                device_id={"blk": owner_at(index)}, device_id_type=mesh_id,
-            ).start()
-            return carry
-
-        return step
+    def give(index):
+        pltpu.make_async_remote_copy(
+            src_ref=piece(send1, index), dst_ref=piece(recv1, me), send_sem=a_send, recv_sem=a_recv,
+            device_id={"blk": owner_at(index)}, device_id_type=mesh_id,
+        ).start()
+
+    def to_owner(j, carry):
+        give(lax.rem(mine + 1 + j, 16))
+        return carry
 
     def to_column(column):
         for r in range(4):
@@ -400,7 +399,15 @@
             if bit < 3:
                 signal(met.at[bit + 1], cube(bit + 1))
 
-    lax.fori_loop(0, 16 - owner, to_owner(owner * (mine + 1) + 4 * (1 - owner)), 0)
+    @pl.when(guest)
+    def _():
+        for index in (4, 5, 6, 7, 8, 9, 10, 11, 12, 13, 14, 15, 0, 1, 2, 3):
+            give(index)
+
+    @pl.when(owns)
+    def _():
+        lax.fori_loop(0, 15, to_owner, 0)
+
 
     @pl.when(owner * up == 1)
     def _():

time: 28.6 us -> 28.6 us (level)
  no operation moved by 1% of the time
where the time goes in v6:
time: 28.6 us; the launch traced here: 28.3 us
  Pallas kernels  27.7 us (97%)
  between operations  0.64 us (2%)
    pallas_call x1, Pallas kernels, per_device(): pl.pallas_call(kernel, out_shape=(jax.ShapeDtypeStruct((TILE, 128), f32),...  26.6 us
    pallas_call x1, Pallas kernels, per_device(): pl.pallas_call(tail, out_shape=(jax.ShapeDtypeStruct((768, 32), f32), jax...  1.15 us

profile of v6, /device:TPU:1, one launch (start us, length us, event | category | flops | bytes accessed | tf_op | source)
XLA Modules:
  0.0 28.3 jit_solution(9655459722028557863)
XLA Ops:
  0.6 26.6 %segment.1 = (f32[256,128]{1,0:T(8,128)S(1)}, f32[3,128,256]{2,1,0:T(8,128)S(1)}, f32[3,8,32,256]{3,2,1,0:T(8,128)S(1)}, f32[8,32,256]{2,1,0:T(8,128)S(1)}) custom-call(f32[768,32]{1,0:T(8,128)} %bitcast.4, f32[8,32,256]{2,1,0:T(8,128)} %sc_in.1, s32[1,256]{1,0:T(1,128)} %bitcast.5, f32[1,256]{1,0:T(1,128)} %bitcast.6, bf16[256,4096]{1,0:T(8,128)(2,1)} %constant.2.clone.tab_in), custom_call_target="tpu_custom_call" | custom-call | tf_op jit(solution)/shard_map/segment/pallas_call | solution.py:476
  27.2 1.2 %tail.1 = (f32[768,32]{1,0:T(8,128)}, f32[8,32,256]{2,1,0:T(8,128)}) custom-call(f32[256,128]{1,0:T(8,128)S(1)} %get-tuple-element.8.tiles, f32[3,128,256]{2,1,0:T(8,128)S(1)} %get-tuple-element.9.weights, f32[3,8,32,256]{3,2,1,0:T(8,128)S(1)} %get-tuple-element.10.slopes, f32[8,32,256]{2,1,0:T(8,128)S(1)} %get-tuple-element.11.still), custom_call_target="tpu_custom_call" | custom-call | tf_op jit(solution)/shard_map/tail/pallas_call | solution.py:532
